TPU v7x, 256 devices: a whole 4x4x8 slice. The times are simulated.
256 devices in a mesh: row: 8 (over x_lo, y), col: 32 (over z, x_hi, core).
Axes of the slice: x: 4 (x_hi: 2, x_lo: 2; x = x_hi * 2 + x_lo), y: 4, z: 8, core: 2. Of those that a mesh axis runs over, the one named last changes fastest.
Arguments:
- b_steps: float32 [2, 1024, 8192], P(None, 'row', 'col'), may hold values from -6 to 6
- b_trail: float32 [8192, 8192], P('row', 'col'), may hold values from -6 to 6
- l_cross: float32 [1024, 1024], P('row', 'col'), may hold values from -0.1875 to 0.1875
- l_trail: float32 [2, 8192, 1024], P(None, 'row', 'col'), may hold values from -0.125 to 0.125
- diag_inv: float32 [2, 2, 512, 512], P(None, None, None, 'col'), may hold values from -1.5 to 1.5, as said below
- diag_low: float32 [2, 512, 512], P(None, None, 'col'), may hold values from -0.25 to 0.25
Outputs:
- x_steps: float32 [2, 1024, 8192], P(None, 'row', 'col')
- trail_out: float32 [8192, 8192], P('row', 'col')
Inputs may be any that keep to these rules, and one draw needn't show every extreme that they name: Each diag_inv[s, h] is lower triangular with diagonal entries of 0.5 to 1.5 and strictly lower entries of magnitude at most 3 / sqrt(512).
All inputs are finite; a program needn't handle non-finite values.
Results may differ from a plain program's by a relative error of at most 0.00013.
Values sent between devices are 32-bit elements; how exact they have to be, the bound alone decides.
A program may use at most 64 MiB of HBM per device.

v0:
```python
import jax
import jax.numpy as jnp
from jax import lax
from jax.sharding import PartitionSpec as P

exact_prec = lax.Precision.HIGHEST


def mult(left_mat, right_mat):
    return jnp.dot(left_mat, right_mat, precision=exact_prec, preferred_element_type=jnp.float32)


def inverse_columns(diag_inv, diag_low, section, offset, own_rows):
    inv_first = diag_inv[section, 0]
    inv_second = diag_inv[section, 1]
    low_block = diag_low[section]
    second_all, low_all = (
        lax.all_gather(inv_second, "col", axis=1, tiled=True),
        lax.all_gather(low_block, "col", axis=1, tiled=True),
    )
    left_cols = jnp.concatenate([inv_first, -mult(second_all, mult(low_all, inv_first))], 0)
    right_cols = jnp.concatenate([jnp.zeros_like(inv_second), inv_second], 0)
    left_all, right_all = (
        lax.all_gather(left_cols, "col", axis=1, tiled=True),
        lax.all_gather(right_cols, "col", axis=1, tiled=True),
    )
    whole = jnp.concatenate([left_all, right_all], 1)
    return lax.dynamic_slice_in_dim(whole, offset, own_rows, 1)


def solve_step(diag_inv, diag_low, section, offset, own_rows, rows_block):
    inverse_cols = inverse_columns(diag_inv, diag_low, section, offset, own_rows)
    return lax.psum(mult(inverse_cols, rows_block), "row")


def shards(b_steps, b_trail, l_cross, l_trail, diag_inv, diag_low):
    own_rows = b_steps.shape[1]
    offset = lax.axis_index("row") * own_rows
    solved_first = solve_step(diag_inv, diag_low, 0, offset, own_rows, b_steps[0])
    segment = solved_first
    next_rows = b_steps[1] - mult(lax.all_gather(l_cross, "col", axis=1, tiled=True), segment)
    trail = b_trail - mult(lax.all_gather(l_trail[0], "col", axis=1, tiled=True), segment)
    solved_second = solve_step(diag_inv, diag_low, 1, offset, own_rows, next_rows)
    segment = solved_second
    trail = trail - mult(lax.all_gather(l_trail[1], "col", axis=1, tiled=True), segment)
    mine_first = lax.dynamic_slice_in_dim(solved_first, offset, own_rows, 0)
    mine_second = lax.dynamic_slice_in_dim(solved_second, offset, own_rows, 0)
    return (jnp.stack([mine_first, mine_second]), trail)


def solution(mesh):
    placed = (
        P(None, "row", "col"),
        P("row", "col"),
        P("row", "col"),
        P(None, "row", "col"),
        P(None, None, None, "col"),
        P(None, None, "col"),
    )
    return jax.shard_map(
        shards,
        mesh=mesh,
        in_specs=placed,
        out_specs=(P(None, "row", "col"), P("row", "col")),
        check_vma=False,
    )
```

profile of v0, /device:TPU:1, one launch (start us, length us, event | category | flops | bytes accessed | tf_op | source)
XLA Modules:
  0.0 1003.2 jit_solution(6268098617561068982)
XLA Ops:
  7.2 1.4 fusion.38
  8.7 1.4 slice_bitcast_fusion.4
  10.9 82.2 %all-gather.25.cloned.1.call-done = f32[1,512,512]{1,2,0:T(8,128)} async-done(((f32[1,512,16]{1,2,0:T(8,128)}), f32[1,512,512]{1,2,0:T(8,128)}) %all-gather.25.cloned.1.call-update) | async-done | bytes 1048592 | tf_op jit(solution)/shard_map/all_gather | solution.py:19
  93.1 3.0 fusion.23
  96.2 74.2 %all-gather.27.cloned.1.call-done = f32[1,1,512,512]{2,3,1,0:T(8,128)} async-done(((f32[1,1,512,16]{2,3,1,0:T(8,128)}), f32[1,1,512,512]{2,3,1,0:T(8,128)}) %all-gather.27.cloned.1.call-update) | async-done | bytes 1048592 | tf_op jit(solution)/shard_map/all_gather | solution.py:18
  170.4 1.8 fusion.18
  174.1 76.5 %all-gather.19.cloned.1.call-done = f32[1024,512]{0,1:T(8,128)} async-done(((f32[1024,16]{0,1:T(8,128)}), f32[1024,512]{0,1:T(8,128)}) %all-gather.19.cloned.1.call-update) | async-done | bytes 2097168 | tf_op jit(solution)/shard_map/all_gather | solution.py:25
  250.6 79.8 %all-gather.17.cloned.1.call-done = f32[1024,512]{0,1:T(8,128)} async-done(((f32[1024,16]{0,1:T(8,128)}), f32[1024,512]{0,1:T(8,128)}) %all-gather.17.cloned.1.call-update) | async-done | bytes 2097168 | tf_op jit(solution)/shard_map/all_gather | solution.py:24
  330.4 3.1 fusion.29
  334.3 72.9 %all-gather.29.cloned.1.call-done = f32[1,512,512]{1,2,0:T(8,128)} async-done(((f32[1,512,16]{1,2,0:T(8,128)}), f32[1,512,512]{1,2,0:T(8,128)}) %all-gather.29.cloned.1.call-update) | async-done | bytes 1048592 | tf_op jit(solution)/shard_map/all_gather | solution.py:19
  407.2 3.0 fusion.20
  410.3 74.1 %all-gather.31.cloned.1.call-done = f32[1,1,512,512]{2,3,1,0:T(8,128)} async-done(((f32[1,1,512,16]{2,3,1,0:T(8,128)}), f32[1,1,512,512]{2,3,1,0:T(8,128)}) %all-gather.31.cloned.1.call-update) | async-done | bytes 1048592 | tf_op jit(solution)/shard_map/all_gather | solution.py:18
  484.3 1.8 fusion.17
  487.7 40.3 %all_gather.41 = f32[128,1024]{0,1:T(8,128)S(1)} all-gather(f32[128,32]{0,1:T(8,128)S(1)} %copy-done.4), channel_id=1, replica_groups=mesh['row'=8,'col'=32] {'col'}, dimensions={1}, use_global_device_ids=true | all-gather | bytes 540672 | tf_op jit(solution)/shard_map/all_gather | solution.py:41
  527.9 34.2 %all-reduce.5.cloned.1.call-done = f32[1024,256]{1,0:T(8,128)} async-done(((f32[1024,256]{1,0:T(8,128)}), f32[1024,256]{1,0:T(8,128)}) %all-reduce.5.cloned.1.call-update) | async-done | bytes 1048592 | tf_op jit(solution)/shard_map/psum | solution.py:33
  562.1 2.2 fusion.16
  564.4 85.6 %all-gather.23.cloned.1.call-done = f32[1024,512]{0,1:T(8,128)} async-done(((f32[1024,16]{0,1:T(8,128)}), f32[1024,512]{0,1:T(8,128)}) %all-gather.23.cloned.1.call-update) | async-done | bytes 2097168 | tf_op jit(solution)/shard_map/all_gather | solution.py:25
  649.9 79.4 %all-gather.21.cloned.1.call-done = f32[1024,512]{0,1:T(8,128)} async-done(((f32[1024,16]{0,1:T(8,128)}), f32[1024,512]{0,1:T(8,128)}) %all-gather.21.cloned.1.call-update) | async-done | bytes 2097168 | tf_op jit(solution)/shard_map/all_gather | solution.py:24
  729.3 3.0 fusion.26
  733.3 82.1 %all-gather.35.cloned.1.call-done = f32[1,1024,1024]{1,2,0:T(8,128)} async-done(((f32[1,1024,32]{1,2,0:T(8,128)}), f32[1,1024,1024]{1,2,0:T(8,128)}) %all-gather.35.cloned.1.call-update) | async-done | bytes 4194320 | tf_op jit(solution)/shard_map/all_gather | solution.py:45
  815.4 76.7 %all-reduce.7.cloned.1.call-done = f32[1024,256]{1,0:T(8,128)} async-done(((f32[1024,256]{1,0:T(8,128)}), f32[1024,256]{1,0:T(8,128)}) %all-reduce.7.cloned.1.call-update) | async-done | bytes 1048592 | tf_op jit(solution)/shard_map/psum | solution.py:33
  892.2 7.1 fusion.13
  899.2 88.0 %all-gather.33.cloned.1.call-done = f32[1,1024,1024]{1,2,0:T(8,128)} async-done(((f32[1,1024,32]{1,2,0:T(8,128)}), f32[1,1024,1024]{1,2,0:T(8,128)}) %all-gather.33.cloned.1.call-update) | async-done | bytes 4194320 | tf_op jit(solution)/shard_map/all_gather | solution.py:42
  987.3 6.1 fusion.10
  (44 shorter events, 8.9 us)
Async XLA Ops:
  7.2 86.0 %all-gather.25.cloned.1.call-start = ((), (), s32[]{:S(2)}) async-start(), calls=%async_computation.6 | async-start | bytes 1081344 | tf_op jit(solution)/shard_map/all_gather | solution.py:19
  8.6 161.7 %all-gather.27.cloned.1.call-start = ((), (), s32[]{:S(2)}) async-start(), calls=%async_computation.7 | async-start | bytes 1081344 | tf_op jit(solution)/shard_map/all_gather | solution.py:18
  10.2 240.4 %all-gather.19.cloned.1.call-start = ((), (), s32[]{:S(2)}) async-start(), calls=%async_computation.1 | async-start | bytes 2162688 | tf_op jit(solution)/shard_map/all_gather | solution.py:25
  10.9 319.5 %all-gather.17.cloned.1.call-start = ((), (), s32[]{:S(2)}) async-start(), calls=%async_computation | async-start | bytes 2162688 | tf_op jit(solution)/shard_map/all_gather | solution.py:24
  172.9 234.4 %all-gather.29.cloned.1.call-start = ((), (), s32[]{:S(2)}) async-start(), calls=%async_computation.8 | async-start | bytes 1081344 | tf_op jit(solution)/shard_map/all_gather | solution.py:19
  173.5 310.9 %all-gather.31.cloned.1.call-start = ((), (), s32[]{:S(2)}) async-start(), calls=%async_computation.9 | async-start | bytes 1081344 | tf_op jit(solution)/shard_map/all_gather | solution.py:18
  174.0 388.1 %all-reduce.5.cloned.1.call-start = ((), (), s32[]{:S(2)}) async-start(), calls=%async_computation.2 | async-start | bytes 2097152 | tf_op jit(solution)/shard_map/psum | solution.py:33
  174.1 312.8 %copy-start.3 = (f32[2,1024,32]{1,2,0:T(8,128)S(1)}, f32[2,1024,32]{1,2,0:T(8,128)}, u32[]{:S(2)}) copy-start(f32[2,1024,32]{1,2,0:T(8,128)} %param.9) | copy-start | bytes 786436
  174.1 313.6 %copy-start.4 = (f32[128,32]{0,1:T(8,128)S(1)}, f32[128,32]{0,1:T(8,128)}, u32[]{:S(2)}) copy-start(f32[128,32]{0,1:T(8,128)} %param.8) | copy-start | bytes 49156
  174.1 388.0 %copy-start.2 = (f32[2,128,256]{2,1,0:T(8,128)S(1)}, f32[2,128,256]{2,1,0:T(8,128)}, u32[]{:S(2)}) copy-start(f32[2,128,256]{2,1,0:T(8,128)} %param.6) | copy-start | bytes 786436
  333.5 316.4 %all-gather.23.cloned.1.call-start = ((), (), s32[]{:S(2)}) async-start(), calls=%async_computation.4 | async-start | bytes 2162688 | tf_op jit(solution)/shard_map/all_gather | solution.py:25
  334.2 395.1 %all-gather.21.cloned.1.call-start = ((), (), s32[]{:S(2)}) async-start(), calls=%async_computation.3 | async-start | bytes 2162688 | tf_op jit(solution)/shard_map/all_gather | solution.py:24
  486.8 328.6 %all-gather.35.cloned.1.call-start = ((), (), s32[]{:S(2)}) async-start(), calls=%async_computation.11 | async-start | bytes 4325376 | tf_op jit(solution)/shard_map/all_gather | solution.py:45
  487.6 404.5 %all-reduce.7.cloned.1.call-start = ((), (), s32[]{:S(2)}) async-start(), calls=%async_computation.5 | async-start | bytes 2097152 | tf_op jit(solution)/shard_map/psum | solution.py:33
  527.9 205.0 %copy-start.1 = (f32[1024,256]{1,0:T(8,128)S(1)}, f32[1024,256]{1,0:T(8,128)}, u32[]{:S(2)}) copy-start(f32[1024,256]{1,0:T(8,128)} %param.7) | copy-start | bytes 3145732
  564.4 169.0 %copy-start = (f32[1024,256]{1,0:T(8,128)S(1)}, f32[1024,256]{1,0:T(8,128)}, u32[]{:S(2)}) copy-start(f32[1024,256]{1,0:T(8,128)} %all-reduce.5.cloned.1.call-done) | copy-start | bytes 3145732
  732.4 254.9 %all-gather.33.cloned.1.call-start = ((), (), s32[]{:S(2)}) async-start(), calls=%async_computation.10 | async-start | bytes 4325376 | tf_op jit(solution)/shard_map/all_gather | solution.py:42
Sparse Core Ops, SparseCore 0:
  11.4 81.7 all-gather.24
  95.9 74.3 all-gather.26
  173.7 76.8 all-gather.18
  253.8 76.5 all-gather.16
  333.0 74.1 all-gather.28
  409.9 74.3 all-gather.30
  487.5 74.5 all-reduce.4
  564.9 84.9 all-gather.22
  652.7 76.5 all-gather.20
  732.0 83.4 all-gather.34
  818.6 73.4 all-reduce.6
  895.4 91.8 all-gather.32
where the time goes:
time: 1000 us
  waiting for transfers between devices  907 us (91%)
  blocking collectives  40.3 us (4%)
  matrix products  31.2 us (3%)
  between operations  14.3 us (1%)
    all_gather x2, waiting for transfers between devices, inverse_columns(): lax.all_gather(right_cols, 'col', axis=1, tiled=True)  162 us
    all_gather x2, waiting for transfers between devices, inverse_columns(): lax.all_gather(left_cols, 'col', axis=1, tiled=True)  159 us
    all_gather x2, waiting for transfers between devices, inverse_columns(): lax.all_gather(low_block, 'col', axis=1, tiled=True)  155 us
    all_gather x2, waiting for transfers between devices, inverse_columns(): lax.all_gather(inv_second, 'col', axis=1, tiled=True)  148 us
    psum x2, waiting for transfers between devices, solve_step(): return lax.psum(mult(inverse_cols, rows_block), 'row')  111 us
    all_gather x1, waiting for transfers between devices, shards(): lax.all_gather(l_trail[0], 'col', axis=1, tiled=True)  88 us
    all_gather x1, waiting for transfers between devices, shards(): lax.all_gather(l_trail[1], 'col', axis=1, tiled=True)  82.1 us
    all_gather x1, blocking collectives, shards(): lax.all_gather(l_cross, 'col', axis=1, tiled=True)  40.3 us
  transfers between devices with their start and end apart: 12, of which 12 were waited for; matrix products, arithmetic and copies ran while one was open for 3% of the time, Pallas kernels for 0%

commit v1 on v0

v1 whole, which is shorter than its diff:
```python
import jax
import jax.numpy as jnp
from jax import lax
from jax.experimental import pallas as pl
from jax.experimental.pallas import tpu as pltpu
from jax.sharding import PartitionSpec as P

MESH = pl.DeviceIdType.MESH
F32 = jnp.float32
BF16 = jnp.bfloat16

NY, NZ = 4, 8
RING = (0, 1, 7, 2, 6, 3, 5, 4)
N_SEM = 256


def split(value):
    high = value.astype(BF16)
    return high, (value - high.astype(F32)).astype(BF16)


def product(left, right):
    dot = lambda a, b: jnp.dot(a, b, preferred_element_type=F32)
    return dot(left[0], right[0]) + (dot(left[0], right[1]) + dot(left[1], right[0]))


def kernel(
    b_steps, b_trail, cross, trail, inv, low,
    x_out, t_out,
    lf, tab, crs, rhs, xs, acc, bs, bt, xo, to,
    ss, rs, ls, os,
):
    row, col = lax.axis_index("row"), lax.axis_index("col")
    xl, y = row // NY, row % NY
    z, xh, k = col // 4, (col // 2) % 2, col % 2

    def dev(dxl=0, dy=0, dz=0, dxh=0, dk=0):
        a = (1 - xl) if dxl else xl
        b = (1 - xh) if dxh else xh
        c = (1 - k) if dk else k
        return (a * NY + (y + dy) % NY, ((z + dz) % NZ) * 4 + b * 2 + c)

    ids = {}

    def sem(name):
        return ids.setdefault(name, len(ids))

    started = []

    def send(name, src, dst, to_dev):
        i = sem(name)
        copy = pltpu.make_async_remote_copy(
            src_ref=src, dst_ref=dst, send_sem=ss.at[i], recv_sem=rs.at[i],
            device_id=to_dev, device_id_type=MESH)
        copy.start()
        started.append(copy)

    def recv(name, region, from_dev):
        i = sem(name)
        pltpu.make_async_remote_copy(
            src_ref=region, dst_ref=region, send_sem=ss.at[i], recv_sem=rs.at[i],
            device_id=from_dev, device_id_type=MESH).wait_recv()

    partners = [dev(dz=e) for e in range(1, NZ)] + [dev(dy=1), dev(dy=3), dev(dxl=1), dev(dxh=1), dev(dk=1)]
    barrier = pltpu.get_barrier_semaphore()
    for p in partners:
        pl.semaphore_signal(barrier, inc=1, device_id=p, device_id_type=MESH)
    loads = []

    def load(src, dst):
        copy = pltpu.make_async_copy(src, dst, ls.at[len(loads)])
        copy.start()
        loads.append(copy)

    lanes = pl.ds(pl.multiple_of(y * 128, 128), 128)
    load(b_steps, bs)
    load(cross, crs.at[z, k, xh])
    for s in range(2):
        mine = tab.at[s, z, k, y, xh]
        load(inv.at[s, 0, :, lanes], mine.at[pl.ds(0, 16)])
        load(low.at[s, :, lanes], mine.at[pl.ds(16, 16)])
        load(inv.at[s, 1, :, lanes], mine.at[pl.ds(32, 16)])
    for s in range(2):
        load(trail.at[s], lf.at[s, z, k, xh])
    load(b_trail, bt)
    for c in loads[:8]:
        c.wait()
    pl.semaphore_wait(barrier, len(partners))

    def zrel(e):
        return (z + NZ - e) % NZ

    def t_zsend(g):
        for e in range(1, NZ):
            blk = tab.at[g, z, k, y, xh]
            send(("tz", g, e), blk, blk, dev(dz=e))
            if g == 0:
                blk = crs.at[z, k, xh]
                send(("cz", e), blk, blk, dev(dz=e))

    def t_xsend(g, e):
        blk = tab.at[g, zrel(e), k, y, xh]
        if e:
            recv(("tz", g, e), blk, dev(dz=NZ - e))
        send(("tx", g, e), blk, blk, dev(dxh=1))
        if g == 0:
            blk = crs.at[zrel(e), k, xh]
            if e:
                recv(("cz", e), blk, dev(dz=NZ - e))
            send(("cx", e), blk, blk, dev(dxh=1))

    def t_ysend(g, e):
        recv(("tx", g, e), tab.at[g, zrel(e), k, y, 1 - xh], dev(dxh=1))
        blk = tab.at[g, zrel(e), k, y]
        send(("ty+", g, e), blk, blk, dev(dy=1))
        send(("ty-", g, e), blk, blk, dev(dy=3))

    def t_yforward(g, e):
        recv(("ty+", g, e), tab.at[g, zrel(e), k, (y + 3) % NY], dev(dy=3))
        blk = tab.at[g, zrel(e), k, (y + 3) % NY, 0]
        send(("tf+", g, e), blk, blk, dev(dy=1))
        recv(("ty-", g, e), tab.at[g, zrel(e), k, (y + 1) % NY], dev(dy=1))
        blk = tab.at[g, zrel(e), k, (y + 1) % NY, 1]
        send(("tf-", g, e), blk, blk, dev(dy=3))

    def t_core(g, e):
        far = (y + 2) % NY
        recv(("tf+", g, e), tab.at[g, zrel(e), k, far, 0], dev(dy=3))
        recv(("tf-", g, e), tab.at[g, zrel(e), k, far, 1], dev(dy=1))
        blk = tab.at[g, zrel(e), k]
        send(("tk", g, e), blk, blk, dev(dk=1))
        if g == 0:
            recv(("cx", e), crs.at[zrel(e), k, 1 - xh], dev(dxh=1))
            blk = crs.at[zrel(e), k]
            send(("ck", e), blk, blk, dev(dk=1))

    def t_done(g, e):
        recv(("tk", g, e), tab.at[g, zrel(e), 1 - k], dev(dk=1))
        if g == 0:
            recv(("ck", e), crs.at[zrel(e), 1 - k], dev(dk=1))

    def l_hop(s, h):
        for sign, last in ((1, 4 if s == 0 else 3), (-1, 3 if s == 0 else 4)):
            if h > last:
                continue
            at = zrel(h if sign > 0 else NZ - h)
            blk = lf.at[s, at, k] if s == 0 else lf.at[s, at, k, xh]
            if h:
                recv(("l", s, sign, h), blk, dev(dz=NZ - sign))
            if h < last:
                send(("l", s, sign, h + 1), blk, blk, dev(dz=sign % NZ))
            if h == 0 and sign < 0:
                continue
            if s == 0:
                send(("lk", s, sign * h), blk, blk, dev(dk=1))
            else:
                send(("lx", s, sign * h), blk, blk, dev(dxh=1))

    def l_cross(s, h):
        for sign, last in ((1, 3), (-1, 4)):
            if h > last or (h == 0 and sign < 0):
                continue
            at = zrel(h if sign > 0 else NZ - h)
            recv(("lx", s, sign * h), lf.at[s, at, k, 1 - xh], dev(dxh=1))
            blk = lf.at[s, at, k]
            send(("lk", s, sign * h), blk, blk, dev(dk=1))

    def l_done(s, h):
        for sign, last in ((1, 4 if s == 0 else 3), (-1, 3 if s == 0 else 4)):
            if h > last or (h == 0 and sign < 0):
                continue
            at = zrel(h if sign > 0 else NZ - h)
            recv(("lk", s, sign * h), lf.at[s, at, 1 - k], dev(dk=1))

    def r_send(g):
        blk = rhs.at[g, xl, y]
        send(("rx", g), blk, blk, dev(dxl=1))
        send(("ry+", g, 0), blk, blk, dev(dy=1))
        send(("ry-", g, 0), blk, blk, dev(dy=3))

    def r_other(g):
        blk = rhs.at[g, 1 - xl, y]
        recv(("rx", g), blk, dev(dxl=1))
        send(("ry+", g, 1), blk, blk, dev(dy=1))
        send(("ry-", g, 1), blk, blk, dev(dy=3))

    def r_forward(g):
        for j in range(2):
            which = xl if j == 0 else 1 - xl
            recv(("ry+", g, j), rhs.at[g, which, (y + 3) % NY], dev(dy=3))
            recv(("ry-", g, j), rhs.at[g, which, (y + 1) % NY], dev(dy=1))
            if j == 0:
                blk = rhs.at[g, which, (y + 3) % NY]
                send(("rf", g, j), blk, blk, dev(dy=1))
            else:
                blk = rhs.at[g, which, (y + 1) % NY]
                send(("rf", g, j), blk, blk, dev(dy=3))

    def r_done(g):
        far = (y + 2) % NY
        recv(("rf", g, 0), rhs.at[g, xl, far], dev(dy=3))
        recv(("rf", g, 1), rhs.at[g, 1 - xl, far], dev(dy=1))

    places = [(a, c, b) for a in range(NZ) for b in range(2) for c in range(2)]

    def weights(s, which, pair):
        halves = [
            jnp.concatenate([tab[s, a, c, 2 * pair + j, b, 16 * which:16 * which + 16, :] for a, c, b in places], axis=0)
            for j in range(2)
        ]
        return split(jnp.concatenate(halves, axis=1))

    def solve(s):
        top = split(jnp.concatenate([rhs[s, 0, j] for j in range(4)], axis=1))
        for pair in range(2):
            out = product(top, weights(s, 0, pair))
            xs[s, 2 * pair] = out[:, :128]
            xs[s, 2 * pair + 1] = out[:, 128:]
        first = split(jnp.concatenate([xs[s, j] for j in range(4)], axis=1))
        rest = []
        for pair in range(2):
            out = product(first, weights(s, 1, pair))
            rest.append(rhs[s, 1, 2 * pair] - out[:, :128])
            rest.append(rhs[s, 1, 2 * pair + 1] - out[:, 128:])
        rest = split(jnp.concatenate(rest, axis=1))
        for pair in range(2):
            out = product(rest, weights(s, 2, pair))
            xs[s, 4 + 2 * pair] = out[:, :128]
            xs[s, 5 + 2 * pair] = out[:, 128:]

    def whole(s):
        return split(jnp.concatenate([xs[s, j] for j in range(8)], axis=1))

    def emit(s):
        xo[s] = xs[s, row].T
        copy = pltpu.make_async_copy(xo.at[s], x_out.at[s], os.at[s])
        copy.start()
        return copy

    t_zsend(0)
    rhs[0, xl, y] = bs[0].T
    r_send(0)
    t_xsend(0, 0)
    for c in loads[8:10]:
        c.wait()
    own = lf.at[0, z, k, xh]
    send(("l0x",), own, own, dev(dxh=1))
    l_hop(1, 0)
    r_other(0)
    recv(("l0x",), lf.at[0, z, k, 1 - xh], dev(dxh=1))
    l_hop(0, 0)
    t_zsend(1)
    r_forward(0)
    for i in range(NZ + 4):
        if 0 < i < NZ:
            t_xsend(0, RING[i])
        if 0 <= i - 1 < NZ:
            t_ysend(0, RING[i - 1])
        if 0 <= i - 2 < NZ:
            t_yforward(0, RING[i - 2])
        if 0 <= i - 3 < NZ:
            t_core(0, RING[i - 3])
        if i == 4:
            l_hop(1, 1)
            l_cross(1, 0)
        if i == 6:
            l_hop(0, 1)
        if i == 9:
            l_hop(1, 2)
            l_cross(1, 1)
        if i == 11:
            l_hop(0, 2)
    r_done(0)
    for e in RING:
        t_done(0, e)
    solve(0)
    low_cross = split(jnp.concatenate([crs[a, c, b] for a, c, b in places], axis=0))
    rhs[1, xl, y] = bs[1].T - product(whole(0), low_cross)
    r_send(1)
    copies = [emit(0)]
    r_other(1)
    for i in range(NZ + 4):
        if i < NZ:
            t_xsend(1, RING[i])
        if 0 <= i - 1 < NZ:
            t_ysend(1, RING[i - 1])
        if 0 <= i - 2 < NZ:
            t_yforward(1, RING[i - 2])
        if 0 <= i - 3 < NZ:
            t_core(1, RING[i - 3])
        if i == 3:
            r_forward(1)
        if i == 6:
            l_hop(1, 3)
            l_cross(1, 2)
        if i == 9:
            l_hop(0, 3)
    r_done(1)
    l_hop(1, 4)
    l_cross(1, 3)
    l_hop(0, 4)
    l_cross(1, 4)
    for h in range(5):
        l_done(0, h)

    def tile(s, j):
        at = pl.ds(pl.multiple_of(j * 256, 256), 256)
        return split(jnp.concatenate([lf[s, a, c, b, :, at] for a, c, b in places], axis=0))

    first = whole(0)

    @pl.loop(0, 4)
    def _(j):
        acc[j] = product(first, tile(0, j))

    for e in RING:
        t_done(1, e)
    solve(1)
    copies.append(emit(1))
    for h in range(5):
        l_done(1, h)
    second = whole(1)
    loads[10].wait()

    @pl.loop(0, 4)
    def _(j):
        at = pl.ds(pl.multiple_of(j * 256, 256), 256)
        to[at, :] = bt[at, :] - (acc[j] + product(second, tile(1, j))).T

    last = pltpu.make_async_copy(to, t_out, os.at[2])
    last.start()
    for c in copies:
        c.wait()
    last.wait()
    for c in started:
        c.wait_send()
    assert len(ids) <= N_SEM


def shards(b_steps, b_trail, cross, trail, inv, low):
    anywhere = pl.BlockSpec(memory_space=pl.ANY)
    return pl.pallas_call(
        kernel,
        out_shape=(
            jax.ShapeDtypeStruct((2, 128, 256), F32),
            jax.ShapeDtypeStruct((1024, 256), F32),
        ),
        in_specs=[anywhere] * 6,
        out_specs=(anywhere, anywhere),
        scratch_shapes=[
            pltpu.VMEM((2, NZ, 2, 2, 32, 1024), F32),
            pltpu.VMEM((2, NZ, 2, NY, 2, 48, 128), F32),
            pltpu.VMEM((NZ, 2, 2, 32, 128), F32),
            pltpu.VMEM((2, 2, NY, 256, 128), F32),
            pltpu.VMEM((2, 8, 256, 128), F32),
            pltpu.VMEM((4, 256, 256), F32),
            pltpu.VMEM((2, 128, 256), F32),
            pltpu.VMEM((1024, 256), F32),
            pltpu.VMEM((2, 128, 256), F32),
            pltpu.VMEM((1024, 256), F32),
            pltpu.SemaphoreType.DMA((N_SEM,)),
            pltpu.SemaphoreType.DMA((N_SEM,)),
            pltpu.SemaphoreType.DMA((16,)),
            pltpu.SemaphoreType.DMA((4,)),
        ],
        compiler_params=pltpu.CompilerParams(
            collective_id=0, has_side_effects=True, vmem_limit_bytes=56 << 20),
    )(
        b_steps, b_trail, cross.T, jnp.swapaxes(trail, 1, 2),
        jnp.swapaxes(inv, 2, 3), jnp.swapaxes(low, 1, 2),
    )


def solution(mesh):
    placed = (
        P(None, "row", "col"),
        P("row", "col"),
        P("row", "col"),
        P(None, "row", "col"),
        P(None, None, None, "col"),
        P(None, None, "col"),
    )
    return jax.shard_map(
        shards,
        mesh=mesh,
        in_specs=placed,
        out_specs=(P(None, "row", "col"), P("row", "col")),
        check_vma=False,
    )
```

time: 1000 us -> 113 us (0.11)
  waiting for transfers between devices: 907 us -> 0 us
  Pallas kernels: 0 us -> 107 us
  blocking collectives: 40.3 us -> 0 us
  matrix products: 31.2 us -> 0 us
  between operations: 14.3 us -> 0.64 us
    all_gather x10 -> x0, waiting for transfers between devices: 795 us -> none  [the longest x2 162 us: inverse_columns(): lax.all_gather(right_cols, 'col', axis=1, tiled=True)]
    psum x2 -> x0, waiting for transfers between devices: 111 us -> none  [solve_step(): return lax.psum(mult(inverse_cols, rows_block), 'row')]
    pallas_call x0 -> x1, Pallas kernels: none -> 107 us  [shards(): pl.pallas_call(kernel, out_shape=(jax.ShapeDtypeStruct((2, 128, 256), F32...]
    all_gather x1 -> x0, blocking collectives: 40.3 us -> none  [shards(): lax.all_gather(l_cross, 'col', axis=1, tiled=True)]
    dot_general x9 -> x0, matrix products: 31.2 us -> none  [mult(): jnp.dot(left_mat, right_mat, precision=exact_prec, preferred_element_type...]
  transfers between devices with their start and end apart: 12 -> 0, of which waited for: 12 -> 0; matrix products, arithmetic and copies ran while one was open for 3% -> 0% of each run, Pallas kernels for 0% -> 0%
where the time goes in v1:
time: 113 us; the launch traced here: 111 us
  Pallas kernels  107 us (95%)
  local copies, waits for them, and re-layouts  3.93 us (3%)
    pallas_call x1, Pallas kernels, shards(): pl.pallas_call(kernel, out_shape=(jax.ShapeDtypeStruct((2, 128, 256), F32...  107 us
    unnamed x2, local copies, waits for them, and re-layouts  3.93 us

profile of v1, /device:TPU:1, one launch (start us, length us, event | category | flops | bytes accessed | tf_op | source)
XLA Modules:
  0.0 111.1 jit_solution(1904206680458144988)
XLA Ops:
  0.6 106.5 %shard_map.77 = (f32[2,128,256]{2,1,0:T(8,128)}, f32[1024,256]{1,0:T(8,128)}) custom-call(f32[2,128,256]{2,1,0:T(8,128)} %b_steps.1, f32[1024,256]{1,0:T(8,128)} %b_trail.1, f32[32,128]{1,0:T(8,128)} %bitcast.7, f32[2,32,1024]{2,1,0:T(8,128)} %bitcast.4, f32[2,2,16,512]{3,2,1,0:T(8,128)} %bitcast.5, f32[2,16,512]{2,1,0:T(8,128)} %bitcast.6), custom_call_target="tpu_custom_call" | custom-call | tf_op jit(solution)/shard_map/pallas_call | solution.py:342
  107.2 1.7 %copy.10 = f32[2,128,256]{2,1,0:T(8,128)} copy(f32[2,128,256]{2,1,0:T(8,128)} %get-tuple-element.4) | data formatting | bytes 524288
  108.8 2.3 %copy.11 = f32[1024,256]{1,0:T(8,128)} copy(f32[1024,256]{1,0:T(8,128)} %get-tuple-element.5) | data formatting | bytes 2097152

commit v2 on v1

v2 whole, which is shorter than its diff:
```python
import jax
import jax.numpy as jnp
from jax import lax
from jax.experimental import pallas as pl
from jax.experimental.pallas import tpu as pltpu
from jax.sharding import PartitionSpec as P

MESH = pl.DeviceIdType.MESH
F32 = jnp.float32
BF16 = jnp.bfloat16

NY, NZ = 4, 8
PAIRS = (0, 1, 3, 2)
N_SEND, N_RECV = 32, 128


def split(value):
    high = value.astype(BF16)
    return high, (value - high.astype(F32)).astype(BF16)


def product(left, right):
    dot = lambda a, b: jnp.dot(a, b, preferred_element_type=F32)
    return dot(left[0], right[0]) + (dot(left[0], right[1]) + dot(left[1], right[0]))


def kernel(
    b_steps, b_trail, cross, trail, inv, low,
    x_out, t_out,
    lf, tab, crs, rhs, xs, acc, bs, bt, xo, to,
    ss, rs, ls, os,
):
    row, col = lax.axis_index("row"), lax.axis_index("col")
    xl, y = row // NY, row % NY
    z, xh, k = col // 4, (col // 2) % 2, col % 2

    def dev(dxl=0, dy=0, dz=0, dxh=0, dk=0):
        a = (1 - xl) if dxl else xl
        b = (1 - xh) if dxh else xh
        c = (1 - k) if dk else k
        return (a * NY + (y + dy) % NY, ((z + dz) % NZ) * 4 + b * 2 + c)

    ids, streams = {}, {}

    def sem(name):
        return ids.setdefault(name, len(ids))

    def out_sem(stream):
        return streams.setdefault(stream, len(streams))

    def send(stream, at, src, dst, to_dev):
        pltpu.make_async_remote_copy(
            src_ref=src, dst_ref=dst, send_sem=ss.at[out_sem(stream)],
            recv_sem=rs.at[sem(stream) if at is None else sem((stream, at))],
            device_id=to_dev, device_id_type=MESH).start()

    def recv(stream, at, region, from_dev):
        i = sem(stream) if at is None else sem((stream, at)) if isinstance(at, tuple) else at
        pltpu.make_async_remote_copy(
            src_ref=region, dst_ref=region, send_sem=ss.at[out_sem(stream)], recv_sem=rs.at[i],
            device_id=from_dev, device_id_type=MESH).wait_recv()

    def sent(stream, region):
        pltpu.make_async_remote_copy(
            src_ref=region, dst_ref=region, send_sem=ss.at[streams[stream]], recv_sem=rs.at[0],
            device_id=dev(dk=1), device_id_type=MESH).wait_send()

    partners = [dev(dz=e) for e in range(1, NZ)] + [dev(dy=1), dev(dy=3), dev(dxl=1), dev(dxh=1), dev(dk=1)]
    barrier = pltpu.get_barrier_semaphore()
    for p in partners:
        pl.semaphore_signal(barrier, inc=1, device_id=p, device_id_type=MESH)
    loads = []

    def load(src, dst):
        copy = pltpu.make_async_copy(src, dst, ls.at[len(loads)])
        copy.start()
        loads.append(copy)

    lanes = pl.ds(pl.multiple_of(y * 128, 128), 128)
    load(b_steps, bs)
    load(cross, crs.at[k, xh, z])
    for s in range(2):
        mine = tab.at[s, k, z, y, xh]
        load(inv.at[s, 0, :, lanes], mine.at[pl.ds(0, 16)])
        load(low.at[s, :, lanes], mine.at[pl.ds(16, 16)])
        load(inv.at[s, 1, :, lanes], mine.at[pl.ds(32, 16)])
    for s in range(2):
        load(trail.at[s], lf.at[s, z, k, xh])
    load(b_trail, bt)
    for c in loads[:8]:
        c.wait()
    pl.semaphore_wait(barrier, len(partners))

    def pair(d):
        return (z // 2 + d) % (NZ // 2)

    tz = [[sem(("tz", g, e)) for e in range(NZ)] for g in range(2)]

    def t_zsend(g):
        blk = tab.at[g, k, z, y, xh]
        for e in range(1, NZ):
            pltpu.make_async_remote_copy(
                src_ref=blk, dst_ref=blk, send_sem=ss.at[out_sem(("tz", g))], recv_sem=rs.at[tz[g][e]],
                device_id=dev(dz=e), device_id_type=MESH).start()

    def t_x(g, d):
        zz = pair(d)
        for from_z in [2 * zz, 2 * zz + 1] if d else [z + 1 - 2 * (z % 2)]:
            e = (z - from_z + NZ) % NZ
            recv(("tz", g), tz[g][0] + e, tab.at[g, k, from_z, y, xh], dev(dz=1))
        blk = tab.at[g, k, pl.ds(2 * zz, 2), y, xh]
        send(("tx", g), (d,), blk, blk, dev(dxh=1))

    def t_y(g, d):
        zs = pl.ds(2 * pair(d), 2)
        recv(("tx", g), (d,), tab.at[g, k, zs, y, 1 - xh], dev(dxh=1))
        blk = tab.at[g, k, zs, y]
        send(("ty+", g), (d,), blk, blk, dev(dy=1))
        send(("ty-", g), (d,), blk, blk, dev(dy=3))

    def t_f(g, d):
        zs = pl.ds(2 * pair(d), 2)
        recv(("ty+", g), (d,), tab.at[g, k, zs, (y + 3) % NY], dev(dy=3))
        blk = tab.at[g, k, zs, (y + 3) % NY, 0]
        send(("tf+", g), (d,), blk, blk, dev(dy=1))
        recv(("ty-", g), (d,), tab.at[g, k, zs, (y + 1) % NY], dev(dy=1))
        blk = tab.at[g, k, zs, (y + 1) % NY, 1]
        send(("tf-", g), (d,), blk, blk, dev(dy=3))

    def t_k(g, d):
        zs = pl.ds(2 * pair(d), 2)
        far = (y + 2) % NY
        recv(("tf+", g), (d,), tab.at[g, k, zs, far, 0], dev(dy=3))
        recv(("tf-", g), (d,), tab.at[g, k, zs, far, 1], dev(dy=1))
        blk = tab.at[g, k, zs]
        send(("tk", g), None, blk, blk, dev(dk=1))

    def t_done(g):
        recv(("tk", g), None, tab.at[g, 1 - k], dev(dk=1))

    def t_sent(g):
        sent(("tz", g), tab.at[g, k, pl.ds(0, NZ - 1), y, xh])
        sent(("tx", g), tab.at[g, k, :, y, xh])
        for sign in "+-":
            sent(("ty" + sign, g), tab.at[g, k, :, y])
            sent(("tf" + sign, g), tab.at[g, k, :, y, xh])
        sent(("tk", g), tab.at[g, k])

    def c_z():
        blk = crs.at[k, xh, z]
        for e in range(1, NZ):
            send("cz", None, blk, blk, dev(dz=e))

    def c_x():
        recv("cz", None, crs.at[k, xh, pl.ds(0, NZ - 1)], dev(dz=1))
        send("cx", None, crs.at[k, xh], crs.at[k, xh], dev(dxh=1))

    def c_k():
        recv("cx", None, crs.at[k, 1 - xh], dev(dxh=1))
        send("ck", None, crs.at[k], crs.at[k], dev(dk=1))

    def c_done():
        recv("ck", None, crs.at[1 - k], dev(dk=1))

    def c_sent():
        sent("cz", crs.at[k, xh, pl.ds(0, NZ - 1)])
        sent("cx", crs.at[k, xh])
        sent("ck", crs.at[k])

    def zrel(e):
        return (z + NZ - e) % NZ

    def l_hop(s, h):
        for sign, last in ((1, 4 if s == 0 else 3), (-1, 3 if s == 0 else 4)):
            if h > last:
                continue
            at = zrel(h if sign > 0 else NZ - h)
            blk = lf.at[s, at, k] if s == 0 else lf.at[s, at, k, xh]
            if h:
                recv(("l", s), (sign, h), blk, dev(dz=NZ - sign))
            if h < last:
                send(("l", s), (sign, h + 1), blk, blk, dev(dz=sign % NZ))
            if h == 0 and sign < 0:
                continue
            if s == 0:
                send(("lk", s), None, blk, blk, dev(dk=1))
            else:
                send(("lx", s), (sign * h,), blk, blk, dev(dxh=1))

    def l_cross(s, h):
        for sign, last in ((1, 3), (-1, 4)):
            if h > last or (h == 0 and sign < 0):
                continue
            at = zrel(h if sign > 0 else NZ - h)
            recv(("lx", s), (sign * h,), lf.at[s, at, k, 1 - xh], dev(dxh=1))
            blk = lf.at[s, at, k]
            send(("lk", s), None, blk, blk, dev(dk=1))

    def l_done(s):
        recv(("lk", s), None, lf.at[s, :, 1 - k], dev(dk=1))

    def l_sent():
        sent("l0x", lf.at[0, z, k, xh])
        sent(("l", 0), lf.at[0, pl.ds(0, NZ - 1), k])
        sent(("l", 1), lf.at[1, pl.ds(0, NZ - 1), k, xh])
        sent(("lx", 1), lf.at[1, :, k, xh])
        for s in range(2):
            sent(("lk", s), lf.at[s, :, k])

    def r_send(g):
        blk = rhs.at[g, xl, y]
        send(("rx", g), None, blk, blk, dev(dxl=1))
        send(("ry", g), ("+", 0), blk, blk, dev(dy=1))
        send(("ry", g), ("-", 0), blk, blk, dev(dy=3))

    def r_other(g):
        blk = rhs.at[g, 1 - xl, y]
        recv(("rx", g), None, blk, dev(dxl=1))
        send(("ry", g), ("+", 1), blk, blk, dev(dy=1))
        send(("ry", g), ("-", 1), blk, blk, dev(dy=3))

    def r_forward(g):
        for j in range(2):
            which = xl if j == 0 else 1 - xl
            recv(("ry", g), ("+", j), rhs.at[g, which, (y + 3) % NY], dev(dy=3))
            if j == 0:
                blk = rhs.at[g, which, (y + 3) % NY]
                send(("rf", g), (j,), blk, blk, dev(dy=1))
            recv(("ry", g), ("-", j), rhs.at[g, which, (y + 1) % NY], dev(dy=1))
            if j == 1:
                blk = rhs.at[g, which, (y + 1) % NY]
                send(("rf", g), (j,), blk, blk, dev(dy=3))

    def r_done(g):
        far = (y + 2) % NY
        recv(("rf", g), (0,), rhs.at[g, xl, far], dev(dy=3))
        recv(("rf", g), (1,), rhs.at[g, 1 - xl, far], dev(dy=1))

    def r_sent(g):
        sent(("rx", g), rhs.at[g, xl, y])
        sent(("ry", g), rhs.at[g, xl])
        sent(("rf", g), rhs.at[g, xl, pl.ds(0, 2)])

    places = [(a, c, b) for a in range(NZ) for b in range(2) for c in range(2)]

    def weights(s, which, two):
        halves = [
            jnp.concatenate([tab[s, c, a, 2 * two + j, b, 16 * which:16 * which + 16, :] for a, c, b in places], axis=0)
            for j in range(2)
        ]
        return split(jnp.concatenate(halves, axis=1))

    def solve(s):
        top = split(jnp.concatenate([rhs[s, 0, j] for j in range(4)], axis=1))
        for two in range(2):
            out = product(top, weights(s, 0, two))
            xs[s, 2 * two] = out[:, :128]
            xs[s, 2 * two + 1] = out[:, 128:]
        first = split(jnp.concatenate([xs[s, j] for j in range(4)], axis=1))
        rest = []
        for two in range(2):
            out = product(first, weights(s, 1, two))
            rest.append(rhs[s, 1, 2 * two] - out[:, :128])
            rest.append(rhs[s, 1, 2 * two + 1] - out[:, 128:])
        rest = split(jnp.concatenate(rest, axis=1))
        for two in range(2):
            out = product(rest, weights(s, 2, two))
            xs[s, 4 + 2 * two] = out[:, :128]
            xs[s, 5 + 2 * two] = out[:, 128:]

    def whole(s):
        return split(jnp.concatenate([xs[s, j] for j in range(8)], axis=1))

    def emit(s):
        xo[s] = xs[s, row].T
        copy = pltpu.make_async_copy(xo.at[s], x_out.at[s], os.at[s])
        copy.start()
        return copy

    d0, d1, d2, d3 = PAIRS
    t_zsend(0)
    rhs[0, xl, y] = bs[0].T
    r_send(0)
    t_x(0, d0)
    r_other(0)
    t_x(0, d1)
    t_x(0, d2)
    t_x(0, d3)
    for c in loads[8:10]:
        c.wait()
    own = lf.at[0, z, k, xh]
    send("l0x", None, own, own, dev(dxh=1))
    l_hop(1, 0)
    c_z()
    t_y(0, d0)
    r_forward(0)
    t_zsend(1)
    recv("l0x", None, lf.at[0, z, k, 1 - xh], dev(dxh=1))
    l_hop(0, 0)
    t_y(0, d1)
    t_f(0, d0)
    t_y(0, d2)
    t_f(0, d1)
    t_k(0, d0)
    c_x()
    t_y(0, d3)
    t_f(0, d2)
    t_k(0, d1)
    for d in PAIRS:
        t_x(1, d)
    t_f(0, d3)
    t_k(0, d2)
    l_hop(1, 1)
    l_cross(1, 0)
    t_y(1, d0)
    t_y(1, d1)
    c_k()
    t_k(0, d3)
    l_hop(0, 1)
    t_f(1, d0)
    r_done(0)
    t_done(0)
    c_done()
    solve(0)
    low_cross = split(jnp.concatenate([crs[c, b, a] for a, c, b in places], axis=0))
    rhs[1, xl, y] = bs[1].T - product(whole(0), low_cross)
    r_send(1)
    copies = [emit(0)]
    r_other(1)
    l_hop(1, 2)
    l_cross(1, 1)
    t_y(1, d2)
    t_f(1, d1)
    t_k(1, d0)
    r_forward(1)
    l_hop(0, 2)
    t_y(1, d3)
    t_f(1, d2)
    t_k(1, d1)
    t_f(1, d3)
    t_k(1, d2)
    l_hop(1, 3)
    l_cross(1, 2)
    t_k(1, d3)
    l_hop(0, 3)
    r_done(1)
    l_hop(1, 4)
    l_cross(1, 3)
    l_hop(0, 4)
    l_cross(1, 4)
    l_done(0)

    def tile(s, j):
        at = pl.ds(pl.multiple_of(j * 256, 256), 256)
        return split(jnp.concatenate([lf[s, a, c, b, :, at] for a, c, b in places], axis=0))

    first = whole(0)

    @pl.loop(0, 4)
    def _(j):
        acc[j] = product(first, tile(0, j))

    t_done(1)
    solve(1)
    copies.append(emit(1))
    l_done(1)
    second = whole(1)
    loads[10].wait()

    @pl.loop(0, 4)
    def _(j):
        at = pl.ds(pl.multiple_of(j * 256, 256), 256)
        to[at, :] = bt[at, :] - (acc[j] + product(second, tile(1, j))).T

    last = pltpu.make_async_copy(to, t_out, os.at[2])
    last.start()
    for c in copies:
        c.wait()
    last.wait()
    for g in range(2):
        t_sent(g)
        r_sent(g)
    c_sent()
    l_sent()
    assert len(ids) <= N_RECV and len(streams) <= N_SEND, (len(ids), len(streams))


def shards(b_steps, b_trail, cross, trail, inv, low):
    anywhere = pl.BlockSpec(memory_space=pl.ANY)
    return pl.pallas_call(
        kernel,
        out_shape=(
            jax.ShapeDtypeStruct((2, 128, 256), F32),
            jax.ShapeDtypeStruct((1024, 256), F32),
        ),
        in_specs=[anywhere] * 6,
        out_specs=(anywhere, anywhere),
        scratch_shapes=[
            pltpu.VMEM((2, NZ, 2, 2, 32, 1024), F32),
            pltpu.VMEM((2, 2, NZ, NY, 2, 48, 128), F32),
            pltpu.VMEM((2, 2, NZ, 32, 128), F32),
            pltpu.VMEM((2, 2, NY, 256, 128), F32),
            pltpu.VMEM((2, 8, 256, 128), F32),
            pltpu.VMEM((4, 256, 256), F32),
            pltpu.VMEM((2, 128, 256), F32),
            pltpu.VMEM((1024, 256), F32),
            pltpu.VMEM((2, 128, 256), F32),
            pltpu.VMEM((1024, 256), F32),
            pltpu.SemaphoreType.DMA((N_SEND,)),
            pltpu.SemaphoreType.DMA((N_RECV,)),
            pltpu.SemaphoreType.DMA((16,)),
            pltpu.SemaphoreType.DMA((4,)),
        ],
        compiler_params=pltpu.CompilerParams(
            collective_id=0, has_side_effects=True, vmem_limit_bytes=56 << 20),
    )(
        b_steps, b_trail, cross.T, jnp.swapaxes(trail, 1, 2),
        jnp.swapaxes(inv, 2, 3), jnp.swapaxes(low, 1, 2),
    )


def solution(mesh):
    placed = (
        P(None, "row", "col"),
        P("row", "col"),
        P("row", "col"),
        P(None, "row", "col"),
        P(None, None, None, "col"),
        P(None, None, "col"),
    )
    return jax.shard_map(
        shards,
        mesh=mesh,
        in_specs=placed,
        out_specs=(P(None, "row", "col"), P("row", "col")),
        check_vma=False,
    )
```

time: 113 us -> 87.7 us (0.78); the launches traced: 111 us -> 87.5 us
  Pallas kernels: 107 us -> 83 us
    pallas_call x1, Pallas kernels: 107 us -> 83 us  [shards(): pl.pallas_call(kernel, out_shape=(jax.ShapeDtypeStruct((2, 128, 256), F32...]
where the time goes in v2:
time: 87.7 us; the launch traced here: 87.5 us
  Pallas kernels  83 us (95%)
  local copies, waits for them, and re-layouts  3.93 us (4%)
    pallas_call x1, Pallas kernels, shards(): pl.pallas_call(kernel, out_shape=(jax.ShapeDtypeStruct((2, 128, 256), F32...  83 us
    unnamed x2, local copies, waits for them, and re-layouts  3.93 us

profile of v2, /device:TPU:1, one launch (start us, length us, event | category | flops | bytes accessed | tf_op | source)
XLA Modules:
  0.0 87.5 jit_solution(64882492356304268)
XLA Ops:
  0.6 83.0 %shard_map.77 = (f32[2,128,256]{2,1,0:T(8,128)}, f32[1024,256]{1,0:T(8,128)}) custom-call(f32[2,128,256]{2,1,0:T(8,128)} %b_steps.1, f32[1024,256]{1,0:T(8,128)} %b_trail.1, f32[32,128]{1,0:T(8,128)} %bitcast.7, f32[2,32,1024]{2,1,0:T(8,128)} %bitcast.4, f32[2,2,16,512]{3,2,1,0:T(8,128)} %bitcast.5, f32[2,16,512]{2,1,0:T(8,128)} %bitcast.6), custom_call_target="tpu_custom_call" | custom-call | tf_op jit(solution)/shard_map/pallas_call | solution.py:390
  83.6 1.7 %copy.10 = f32[2,128,256]{2,1,0:T(8,128)} copy(f32[2,128,256]{2,1,0:T(8,128)} %get-tuple-element.4) | data formatting | bytes 524288
  85.3 2.3 %copy.11 = f32[1024,256]{1,0:T(8,128)} copy(f32[1024,256]{1,0:T(8,128)} %get-tuple-element.5) | data formatting | bytes 2097152

commit v3 on v2

--- a/solution.py
+++ b/solution.py
@@ -12,6 +12,22 @@
 NY, NZ = 4, 8
 PAIRS = (0, 1, 3, 2)
 N_SEND, N_RECV = 32, 128
+
+ORDER = (
+    ("tz", 0), ("first",), ("rs", 0), ("tx", 0, 0), ("tx", 0, 3), ("tx", 0, 1), ("load",), ("hop", 1, 0, -1), ("cz",),
+    ("rf", 0, 0), ("ro", 0), ("tz", 1), ("tx", 0, 2), ("ty", 0, 0), ("ty", 0, 3), ("ty", 0, 1), ("hop", 1, 1, -1),
+    ("hop", 1, 0, 1), ("tx", 1, 0), ("rf", 0, 1), ("tx", 1, 3), ("cx",), ("pair",), ("hop", 0, 0, 1),
+    ("hop", 0, 0, -1), ("tf", 0, 0, -1), ("ty", 0, 2), ("tx", 1, 1), ("tf", 0, 3, -1), ("tf", 0, 0, 1), ("tx", 1, 2),
+    ("cross", 1, 1, -1), ("tf", 0, 1, -1), ("hop", 1, 1, 1), ("tf", 0, 3, 1), ("hop", 1, 2, -1), ("tf", 0, 1, 1),
+    ("cross", 1, 0, 1), ("ty", 1, 0), ("tf", 0, 2, 1), ("ty", 1, 3), ("hop", 0, 1, 1), ("tk", 0, 0), ("tf", 0, 2, -1),
+    ("tk", 0, 3), ("tk", 0, 1), ("hop", 0, 1, -1), ("ck",), ("hop", 1, 2, 1), ("ty", 1, 1), ("tf", 1, 0, 1),
+    ("tf", 1, 0, -1), ("ty", 1, 2), ("hop", 1, 3, -1), ("tf", 1, 3, -1), ("tf", 1, 3, 1), ("tk", 0, 2),
+    ("cross", 1, 1, 1), ("hop", 0, 2, 1), ("tf", 1, 1, 1), ("tf", 1, 1, -1), ("next",), ("rs", 1), ("hop", 0, 2, -1),
+    ("hop", 1, 3, 1), ("cross", 1, 2, -1), ("tk", 1, 0), ("tf", 1, 2, 1), ("hop", 1, 4, -1), ("tf", 1, 2, -1),
+    ("tk", 1, 3), ("cross", 1, 2, 1), ("tk", 1, 1), ("hop", 0, 3, 1), ("cross", 1, 3, -1), ("rf", 1, 0), ("tk", 1, 2),
+    ("ro", 1), ("hop", 0, 3, -1), ("cross", 1, 3, 1), ("hop", 0, 4, 1), ("rf", 1, 1), ("cross", 1, 4, -1), ("trail",),
+    ("finish",),
+)
 
 
 def split(value):
@@ -118,14 +134,12 @@
         send(("ty+", g), (d,), blk, blk, dev(dy=1))
         send(("ty-", g), (d,), blk, blk, dev(dy=3))
 
-    def t_f(g, d):
+    def t_f(g, d, sign):
         zs = pl.ds(2 * pair(d), 2)
-        recv(("ty+", g), (d,), tab.at[g, k, zs, (y + 3) % NY], dev(dy=3))
-        blk = tab.at[g, k, zs, (y + 3) % NY, 0]
-        send(("tf+", g), (d,), blk, blk, dev(dy=1))
-        recv(("ty-", g), (d,), tab.at[g, k, zs, (y + 1) % NY], dev(dy=1))
-        blk = tab.at[g, k, zs, (y + 1) % NY, 1]
-        send(("tf-", g), (d,), blk, blk, dev(dy=3))
+        name, near, half = ("+", (y + 3) % NY, 0) if sign > 0 else ("-", (y + 1) % NY, 1)
+        recv(("ty" + name, g), (d,), tab.at[g, k, zs, near], dev(dy=NY - sign))
+        blk = tab.at[g, k, zs, near, half]
+        send(("tf" + name, g), (d,), blk, blk, dev(dy=sign % NY))
 
     def t_k(g, d):
         zs = pl.ds(2 * pair(d), 2)
@@ -170,31 +184,34 @@
     def zrel(e):
         return (z + NZ - e) % NZ
 
-    def l_hop(s, h):
-        for sign, last in ((1, 4 if s == 0 else 3), (-1, 3 if s == 0 else 4)):
-            if h > last:
-                continue
-            at = zrel(h if sign > 0 else NZ - h)
-            blk = lf.at[s, at, k] if s == 0 else lf.at[s, at, k, xh]
-            if h:
-                recv(("l", s), (sign, h), blk, dev(dz=NZ - sign))
-            if h < last:
-                send(("l", s), (sign, h + 1), blk, blk, dev(dz=sign % NZ))
-            if h == 0 and sign < 0:
-                continue
-            if s == 0:
-                send(("lk", s), None, blk, blk, dev(dk=1))
-            else:
-                send(("lx", s), (sign * h,), blk, blk, dev(dxh=1))
-
-    def l_cross(s, h):
-        for sign, last in ((1, 3), (-1, 4)):
-            if h > last or (h == 0 and sign < 0):
-                continue
-            at = zrel(h if sign > 0 else NZ - h)
-            recv(("lx", s), (sign * h,), lf.at[s, at, k, 1 - xh], dev(dxh=1))
-            blk = lf.at[s, at, k]
+    def l_load():
+        for c in loads[8:10]:
+            c.wait()
+        own = lf.at[0, z, k, xh]
+        send("l0x", None, own, own, dev(dxh=1))
+
+    def l_pair():
+        recv("l0x", None, lf.at[0, z, k, 1 - xh], dev(dxh=1))
+
+    def l_hop(s, h, sign):
+        at = zrel(h if sign > 0 else NZ - h)
+        blk = lf.at[s, at, k] if s == 0 else lf.at[s, at, k, xh]
+        if h:
+            recv(("l", s), (sign, h), blk, dev(dz=NZ - sign))
+        if h < (4 if (s == 0) == (sign > 0) else 3):
+            send(("l", s), (sign, h + 1), blk, blk, dev(dz=sign % NZ))
+        if h == 0 and sign < 0:
+            return
+        if s == 0:
             send(("lk", s), None, blk, blk, dev(dk=1))
+        else:
+            send(("lx", s), (sign * h,), blk, blk, dev(dxh=1))
+
+    def l_cross(s, h, sign):
+        at = zrel(h if sign > 0 else NZ - h)
+        recv(("lx", s), (sign * h,), lf.at[s, at, k, 1 - xh], dev(dxh=1))
+        blk = lf.at[s, at, k]
+        send(("lk", s), None, blk, blk, dev(dk=1))
 
     def l_done(s):
         recv(("lk", s), None, lf.at[s, :, 1 - k], dev(dk=1))
@@ -219,20 +236,17 @@
         send(("ry", g), ("+", 1), blk, blk, dev(dy=1))
         send(("ry", g), ("-", 1), blk, blk, dev(dy=3))
 
-    def r_forward(g):
-        for j in range(2):
-            which = xl if j == 0 else 1 - xl
-            recv(("ry", g), ("+", j), rhs.at[g, which, (y + 3) % NY], dev(dy=3))
-            if j == 0:
-                blk = rhs.at[g, which, (y + 3) % NY]
-                send(("rf", g), (j,), blk, blk, dev(dy=1))
-            recv(("ry", g), ("-", j), rhs.at[g, which, (y + 1) % NY], dev(dy=1))
-            if j == 1:
-                blk = rhs.at[g, which, (y + 1) % NY]
-                send(("rf", g), (j,), blk, blk, dev(dy=3))
+    def r_f(g, j):
+        near, sign = ((y + 3) % NY, "+") if j == 0 else ((y + 1) % NY, "-")
+        which = xl if j == 0 else 1 - xl
+        blk = rhs.at[g, which, near]
+        recv(("ry", g), (sign, j), blk, dev(dy=3 if j == 0 else 1))
+        send(("rf", g), (j,), blk, blk, dev(dy=1 if j == 0 else 3))
 
     def r_done(g):
         far = (y + 2) % NY
+        recv(("ry", g), ("-", 0), rhs.at[g, xl, (y + 1) % NY], dev(dy=1))
+        recv(("ry", g), ("+", 1), rhs.at[g, 1 - xl, (y + 3) % NY], dev(dy=3))
         recv(("rf", g), (0,), rhs.at[g, xl, far], dev(dy=3))
         recv(("rf", g), (1,), rhs.at[g, 1 - xl, far], dev(dy=1))
 
@@ -277,106 +291,57 @@
         copy.start()
         return copy
 
-    d0, d1, d2, d3 = PAIRS
-    t_zsend(0)
-    rhs[0, xl, y] = bs[0].T
-    r_send(0)
-    t_x(0, d0)
-    r_other(0)
-    t_x(0, d1)
-    t_x(0, d2)
-    t_x(0, d3)
-    for c in loads[8:10]:
-        c.wait()
-    own = lf.at[0, z, k, xh]
-    send("l0x", None, own, own, dev(dxh=1))
-    l_hop(1, 0)
-    c_z()
-    t_y(0, d0)
-    r_forward(0)
-    t_zsend(1)
-    recv("l0x", None, lf.at[0, z, k, 1 - xh], dev(dxh=1))
-    l_hop(0, 0)
-    t_y(0, d1)
-    t_f(0, d0)
-    t_y(0, d2)
-    t_f(0, d1)
-    t_k(0, d0)
-    c_x()
-    t_y(0, d3)
-    t_f(0, d2)
-    t_k(0, d1)
-    for d in PAIRS:
-        t_x(1, d)
-    t_f(0, d3)
-    t_k(0, d2)
-    l_hop(1, 1)
-    l_cross(1, 0)
-    t_y(1, d0)
-    t_y(1, d1)
-    c_k()
-    t_k(0, d3)
-    l_hop(0, 1)
-    t_f(1, d0)
-    r_done(0)
-    t_done(0)
-    c_done()
-    solve(0)
-    low_cross = split(jnp.concatenate([crs[c, b, a] for a, c, b in places], axis=0))
-    rhs[1, xl, y] = bs[1].T - product(whole(0), low_cross)
-    r_send(1)
-    copies = [emit(0)]
-    r_other(1)
-    l_hop(1, 2)
-    l_cross(1, 1)
-    t_y(1, d2)
-    t_f(1, d1)
-    t_k(1, d0)
-    r_forward(1)
-    l_hop(0, 2)
-    t_y(1, d3)
-    t_f(1, d2)
-    t_k(1, d1)
-    t_f(1, d3)
-    t_k(1, d2)
-    l_hop(1, 3)
-    l_cross(1, 2)
-    t_k(1, d3)
-    l_hop(0, 3)
-    r_done(1)
-    l_hop(1, 4)
-    l_cross(1, 3)
-    l_hop(0, 4)
-    l_cross(1, 4)
-    l_done(0)
+    copies = []
 
     def tile(s, j):
         at = pl.ds(pl.multiple_of(j * 256, 256), 256)
         return split(jnp.concatenate([lf[s, a, c, b, :, at] for a, c, b in places], axis=0))
 
-    first = whole(0)
-
-    @pl.loop(0, 4)
-    def _(j):
-        acc[j] = product(first, tile(0, j))
-
-    t_done(1)
-    solve(1)
-    copies.append(emit(1))
-    l_done(1)
-    second = whole(1)
-    loads[10].wait()
-
-    @pl.loop(0, 4)
-    def _(j):
-        at = pl.ds(pl.multiple_of(j * 256, 256), 256)
-        to[at, :] = bt[at, :] - (acc[j] + product(second, tile(1, j))).T
-
-    last = pltpu.make_async_copy(to, t_out, os.at[2])
-    last.start()
-    for c in copies:
-        c.wait()
-    last.wait()
+    def r_first():
+        rhs[0, xl, y] = bs[0].T
+
+    def r_next():
+        r_done(0)
+        t_done(0)
+        c_done()
+        solve(0)
+        low_cross = split(jnp.concatenate([crs[c, b, a] for a, c, b in places], axis=0))
+        rhs[1, xl, y] = bs[1].T - product(whole(0), low_cross)
+
+    def trail_first():
+        copies.append(emit(0))
+        l_done(0)
+        first = whole(0)
+
+        @pl.loop(0, 4)
+        def _(j):
+            acc[j] = product(first, tile(0, j))
+
+    def finish():
+        r_done(1)
+        t_done(1)
+        solve(1)
+        copies.append(emit(1))
+        l_done(1)
+        second = whole(1)
+        loads[10].wait()
+
+        @pl.loop(0, 4)
+        def _(j):
+            at = pl.ds(pl.multiple_of(j * 256, 256), 256)
+            to[at, :] = bt[at, :] - (acc[j] + product(second, tile(1, j))).T
+
+        copies.append(pltpu.make_async_copy(to, t_out, os.at[2]))
+        copies[-1].start()
+        for c in copies:
+            c.wait()
+
+    for step, *at in ORDER:
+        {
+            "tz": t_zsend, "tx": t_x, "ty": t_y, "tf": t_f, "tk": t_k, "cz": c_z, "cx": c_x, "ck": c_k,
+            "load": l_load, "pair": l_pair, "hop": l_hop, "cross": l_cross, "rs": r_send, "ro": r_other, "rf": r_f,
+            "first": r_first, "next": r_next, "trail": trail_first, "finish": finish,
+        }[step](*at)
     for g in range(2):
         t_sent(g)
         r_sent(g)

time: 87.7 us -> 73 us (0.83)
  Pallas kernels: 83 us -> 67.8 us
    pallas_call x1, Pallas kernels: 83 us -> 67.8 us  [shards(): pl.pallas_call(kernel, out_shape=(jax.ShapeDtypeStruct((2, 128, 256), F32...]
where the time goes in v3:
time: 73 us; the launch traced here: 72.4 us
  Pallas kernels  67.8 us (93%)
  local copies, waits for them, and re-layouts  3.93 us (5%)
    pallas_call x1, Pallas kernels, shards(): pl.pallas_call(kernel, out_shape=(jax.ShapeDtypeStruct((2, 128, 256), F32...  67.8 us
    unnamed x2, local copies, waits for them, and re-layouts  3.93 us

profile of v3, /device:TPU:1, one launch (start us, length us, event | category | flops | bytes accessed | tf_op | source)
XLA Modules:
  0.0 72.4 jit_solution(11684873849276715597)
XLA Ops:
  0.6 67.8 %shard_map.77 = (f32[2,128,256]{2,1,0:T(8,128)}, f32[1024,256]{1,0:T(8,128)}) custom-call(f32[2,128,256]{2,1,0:T(8,128)} %b_steps.1, f32[1024,256]{1,0:T(8,128)} %b_trail.1, f32[32,128]{1,0:T(8,128)} %bitcast.7, f32[2,32,1024]{2,1,0:T(8,128)} %bitcast.4, f32[2,2,16,512]{3,2,1,0:T(8,128)} %bitcast.5, f32[2,16,512]{2,1,0:T(8,128)} %bitcast.6), custom_call_target="tpu_custom_call" | custom-call | tf_op jit(solution)/shard_map/pallas_call | solution.py:355
  68.5 1.7 %copy.10 = f32[2,128,256]{2,1,0:T(8,128)} copy(f32[2,128,256]{2,1,0:T(8,128)} %get-tuple-element.4) | data formatting | bytes 524288
  70.2 2.3 %copy.11 = f32[1024,256]{1,0:T(8,128)} copy(f32[1024,256]{1,0:T(8,128)} %get-tuple-element.5) | data formatting | bytes 2097152

commit v4 on v3

v4 whole, which is shorter than its diff:
```python
import jax
import jax.numpy as jnp
from jax import lax
from jax.experimental import pallas as pl
from jax.experimental.pallas import tpu as pltpu
from jax.sharding import PartitionSpec as P

MESH = pl.DeviceIdType.MESH
F32 = jnp.float32
BF16 = jnp.bfloat16

NY, NZ = 4, 8
PAIRS = (0, 1, 3, 2)
N_SEND, N_RECV = 72, 136

ORDER = (
    ("tz", 0), ("first",), ("rs", 0), ("cz",), ("tx", 0, 0), ("tx", 0, 3), ("tx", 0, 1), ("ro", 0, 0), ("tx", 0, 2),
    ("r0", 0), ("ro", 0, 1), ("ty", 0, 0), ("load",), ("hop", 1, 0, -1), ("tz", 1), ("r1", 0, 0), ("ty", 0, 3),
    ("hop", 1, 0, 1), ("cx",), ("ty", 0, 1), ("r1", 0, 1), ("ty", 0, 2), ("tx", 1, 0), ("tx", 1, 3), ("tf", 0, 0, -1),
    ("hop", 1, 1, -1), ("pair",), ("hop", 0, 0, -1), ("hop", 0, 0, 1), ("tx", 1, 1), ("tf", 0, 0, 1),
    ("tf", 0, 3, -1), ("tx", 1, 2), ("tf", 0, 3, 1), ("hop", 1, 1, 1), ("tf", 0, 1, -1), ("cross", 1, 0, 1),
    ("tf", 0, 1, 1), ("hop", 1, 2, -1), ("tf", 0, 2, 1), ("tf", 0, 2, -1), ("ck",), ("tk", 0, 0), ("ty", 1, 0),
    ("tk", 0, 3), ("ty", 1, 3), ("hop", 0, 1, 1), ("tk", 0, 1), ("tk", 0, 2), ("hop", 0, 1, -1), ("tf", 1, 0, 1),
    ("cross", 1, 1, -1), ("hop", 1, 2, 1), ("tf", 1, 0, -1), ("ty", 1, 1), ("next",), ("rs", 1), ("hop", 1, 3, -1),
    ("tk", 1, 0), ("tf", 1, 3, 1), ("ty", 1, 2), ("tf", 1, 3, -1), ("trail", 0), ("cross", 1, 1, 1), ("tf", 1, 1, -1),
    ("tf", 1, 1, 1), ("hop", 0, 2, 1), ("trail", 1), ("r0", 1), ("hop", 0, 2, -1), ("hop", 1, 3, 1),
    ("cross", 1, 2, -1), ("tf", 1, 2, -1), ("tf", 1, 2, 1), ("hop", 1, 4, -1), ("tk", 1, 3), ("cross", 1, 2, 1),
    ("tk", 1, 1), ("ro", 1, 0), ("hop", 0, 3, 1), ("ro", 1, 1), ("tk", 1, 2), ("r1", 1, 0), ("trail", 2),
    ("hop", 0, 3, -1), ("cross", 1, 3, -1), ("r1", 1, 1), ("cross", 1, 3, 1), ("hop", 0, 4, 1), ("cross", 1, 4, -1),
    ("trail", 3), ("finish",),
)


def split(value):
    high = value.astype(BF16)
    return high, (value - high.astype(F32)).astype(BF16)


def product(left, right):
    dot = lambda a, b: jnp.dot(a, b, preferred_element_type=F32)
    return dot(left[0], right[0]) + (dot(left[0], right[1]) + dot(left[1], right[0]))


def kernel(
    b_steps, b_trail, cross, trail, inv, low,
    x_out, t_out,
    lf, tab, crs, rhs, xs, acc, bs, bt,
    ss, rs, ls,
):
    row, col = lax.axis_index("row"), lax.axis_index("col")
    xl, y = lax.div(row, NY), lax.rem(row, NY)
    z, xh, k = lax.div(col, 4), lax.rem(lax.div(col, 2), 2), lax.rem(col, 2)
    ys = [lax.rem(y + i, NY) for i in range(NY)]
    zs_at = [lax.rem(z + i, NZ) for i in range(NZ)]
    pairs = [lax.rem(lax.div(z, 2) + i, NZ // 2) for i in range(NZ // 2)]
    beside = z + 1 - 2 * lax.rem(z, 2)

    def dev(dxl=0, dy=0, dz=0, dxh=0, dk=0):
        a = (1 - xl) if dxl else xl
        b = (1 - xh) if dxh else xh
        c = (1 - k) if dk else k
        return (a * NY + ys[dy % NY], zs_at[dz % NZ] * 4 + b * 2 + c)

    ids, streams = {}, {}

    def sem(name):
        return ids.setdefault(name, len(ids))

    def out_sem(stream):
        return streams.setdefault(stream, len(streams))

    def send(stream, at, src, dst, to_dev):
        pltpu.make_async_remote_copy(
            src_ref=src, dst_ref=dst, send_sem=ss.at[out_sem(stream)],
            recv_sem=rs.at[sem(stream) if at is None else sem((stream, at))],
            device_id=to_dev, device_id_type=MESH).start()

    def recv(stream, at, region, from_dev):
        i = sem(stream) if at is None else sem((stream, at)) if isinstance(at, tuple) else at
        pltpu.make_async_remote_copy(
            src_ref=region, dst_ref=region, send_sem=ss.at[out_sem(stream)], recv_sem=rs.at[i],
            device_id=from_dev, device_id_type=MESH).wait_recv()

    def sent(stream, region):
        pltpu.make_async_remote_copy(
            src_ref=region, dst_ref=region, send_sem=ss.at[streams[stream]], recv_sem=rs.at[0],
            device_id=dev(dk=1), device_id_type=MESH).wait_send()

    partners = [dev(dz=e) for e in range(1, NZ)] + [dev(dy=1), dev(dy=3), dev(dxl=1), dev(dxh=1), dev(dk=1)]
    barrier = pltpu.get_barrier_semaphore()
    for p in partners:
        pl.semaphore_signal(barrier, inc=1, device_id=p, device_id_type=MESH)
    loads = []

    def load(src, dst):
        copy = pltpu.make_async_copy(src, dst, ls.at[len(loads)])
        copy.start()
        loads.append(copy)

    lanes = pl.ds(pl.multiple_of(y * 128, 128), 128)
    load(b_steps, bs)
    load(cross, crs.at[k, xh, z])
    for s in range(2):
        mine = tab.at[s, k, z, y, xh]
        load(inv.at[s, 0, :, lanes], mine.at[pl.ds(0, 16)])
        load(low.at[s, :, lanes], mine.at[pl.ds(16, 16)])
        load(inv.at[s, 1, :, pl.ds(pl.multiple_of((NY - 1 - y) * 128, 128), 128)], mine.at[pl.ds(32, 16)])
    for s in range(2):
        load(trail.at[s], lf.at[s, z, k, xh])
    load(b_trail, bt)
    for c in loads[:8]:
        c.wait()
    pl.semaphore_wait(barrier, len(partners))

    def filled(zz, at_y, act):
        p, q = zz <= at_y, zz <= NY - 1 - at_y
        for rows, when in (
            (pl.ds(0, 48), p & q),
            (pl.ds(0, 32), p & (zz > NY - 1 - at_y)),
            (pl.ds(16, 32), (zz > at_y) & q),
            (pl.ds(16, 16), (zz > at_y) & (zz > NY - 1 - at_y)),
        ):
            pl.when(when)(lambda rows=rows: act(rows))

    def pair(d):
        return pairs[d]

    tz = [[sem(("tz", g, e)) for e in range(NZ)] for g in range(2)]

    def t_zsend(g):
        def act(rows):
            blk = tab.at[g, k, z, y, xh, rows]
            for e in range(1, NZ):
                pltpu.make_async_remote_copy(
                    src_ref=blk, dst_ref=blk, send_sem=ss.at[out_sem(("tz", g))], recv_sem=rs.at[tz[g][e]],
                    device_id=dev(dz=e), device_id_type=MESH).start()
        filled(pairs[0], y, act)

    def t_x(g, d):
        def act(rows):
            zz = pair(d)
            for from_z in [2 * zz, 2 * zz + 1] if d else [beside]:
                e = lax.rem(z - from_z + NZ, NZ)
                recv(("tz", g), tz[g][0] + e, tab.at[g, k, from_z, y, xh, rows], dev(dz=1))
            blk = tab.at[g, k, pl.ds(2 * zz, 2), y, xh, rows]
            send(("tx", g, d), None, blk, blk, dev(dxh=1))
        filled(pair(d), y, act)

    def t_y(g, d):
        zs = pl.ds(2 * pair(d), 2)

        def act(rows):
            recv(("tx", g, d), None, tab.at[g, k, zs, y, 1 - xh, rows], dev(dxh=1))
            blk = tab.at[g, k, zs, y, :, rows]
            send(("ty+", g, d), None, blk, blk, dev(dy=1))
            send(("ty-", g, d), None, blk, blk, dev(dy=3))
        filled(pair(d), y, act)

    def t_f(g, d, sign):
        zs = pl.ds(2 * pair(d), 2)
        name, near, half = ("+", ys[3], 0) if sign > 0 else ("-", ys[1], 1)

        def act(rows):
            recv(("ty" + name, g, d), None, tab.at[g, k, zs, near, :, rows], dev(dy=NY - sign))
            blk = tab.at[g, k, zs, near, half, rows]
            send(("tf" + name, g, d), None, blk, blk, dev(dy=sign % NY))
        filled(pair(d), near, act)

    def t_k(g, d):
        zs = pl.ds(2 * pair(d), 2)
        far = ys[2]

        def act(rows):
            recv(("tf+", g, d), None, tab.at[g, k, zs, far, 0, rows], dev(dy=3))
            recv(("tf-", g, d), None, tab.at[g, k, zs, far, 1, rows], dev(dy=1))
        filled(pair(d), far, act)
        blk = tab.at[g, k, zs]
        send(("tk", g), None, blk, blk, dev(dk=1))

    def t_done(g):
        recv(("tk", g), None, tab.at[g, 1 - k], dev(dk=1))

    def t_sent(g):
        filled(pairs[0], y, lambda rows: sent(("tz", g), tab.at[g, k, pl.ds(0, NZ - 1), y, xh, rows]))
        for d in PAIRS:
            zs = pl.ds(2 * pair(d), 2)

            def act(rows):
                sent(("tx", g, d), tab.at[g, k, zs, y, xh, rows])
                sent(("ty+", g, d), tab.at[g, k, zs, y, :, rows])
                sent(("ty-", g, d), tab.at[g, k, zs, y, :, rows])
            filled(pair(d), y, act)
            for name, near in (("+", ys[3]), ("-", ys[1])):
                filled(pair(d), near, lambda rows: sent(("tf" + name, g, d), tab.at[g, k, zs, near, 0, rows]))
        sent(("tk", g), tab.at[g, k])

    def c_z():
        blk = crs.at[k, xh, z]
        for e in range(1, NZ):
            send("cz", None, blk, blk, dev(dz=e))

    def c_x():
        recv("cz", None, crs.at[k, xh, pl.ds(0, NZ - 1)], dev(dz=1))
        send("cx", None, crs.at[k, xh], crs.at[k, xh], dev(dxh=1))

    def c_k():
        recv("cx", None, crs.at[k, 1 - xh], dev(dxh=1))
        send("ck", None, crs.at[k], crs.at[k], dev(dk=1))

    def c_done():
        recv("ck", None, crs.at[1 - k], dev(dk=1))

    def c_sent():
        sent("cz", crs.at[k, xh, pl.ds(0, NZ - 1)])
        sent("cx", crs.at[k, xh])
        sent("ck", crs.at[k])

    def zrel(e):
        return zs_at[-e % NZ]

    def l_load():
        for c in loads[8:10]:
            c.wait()
        own = lf.at[0, z, k, xh]
        send("l0x", None, own, own, dev(dxh=1))

    def l_pair():
        recv("l0x", None, lf.at[0, z, k, 1 - xh], dev(dxh=1))

    def l_hop(s, h, sign):
        at = zrel(h if sign > 0 else NZ - h)
        blk = lf.at[s, at, k] if s == 0 else lf.at[s, at, k, xh]
        if h:
            recv(("l", s), (sign, h), blk, dev(dz=NZ - sign))
        if h < (4 if (s == 0) == (sign > 0) else 3):
            send(("l", s), (sign, h + 1), blk, blk, dev(dz=sign % NZ))
        if h == 0 and sign < 0:
            return
        if s == 0:
            send(("lk", s), (sign * h,), blk, blk, dev(dk=1))
        else:
            send(("lx", s), (sign * h,), blk, blk, dev(dxh=1))

    def l_cross(s, h, sign):
        at = zrel(h if sign > 0 else NZ - h)
        recv(("lx", s), (sign * h,), lf.at[s, at, k, 1 - xh], dev(dxh=1))
        blk = lf.at[s, at, k]
        send(("lk", s), None, blk, blk, dev(dk=1))

    def l_done(s):
        recv(("lk", s), None, lf.at[s, :, 1 - k], dev(dk=1))

    def l_sent():
        sent("l0x", lf.at[0, z, k, xh])
        sent(("l", 0), lf.at[0, pl.ds(0, NZ - 1), k])
        sent(("l", 1), lf.at[1, pl.ds(0, NZ - 1), k, xh])
        sent(("lx", 1), lf.at[1, :, k, xh])
        for s in range(2):
            sent(("lk", s), lf.at[s, :, k])

    def r_send(g):
        for h in range(2):
            blk = rhs.at[g, xl, y, h]
            send(("rx", g), (h,), blk, blk, dev(dxl=1))
        blk = rhs.at[g, xl, y]
        send(("ry", g), ("+",), blk, blk, dev(dy=1))
        send(("ry", g), ("-",), blk, blk, dev(dy=3))

    def r_other(g, h):
        blk = rhs.at[g, 1 - xl, y, h]
        recv(("rx", g), (h,), blk, dev(dxl=1))
        send(("ro", g), ("+", h), blk, blk, dev(dy=1))
        send(("ro", g), ("-", h), blk, blk, dev(dy=3))

    def r_f0(g):
        blk = rhs.at[g, xl, ys[3]]
        recv(("ry", g), ("+",), blk, dev(dy=3))
        send(("rf", g), None, blk, blk, dev(dy=1))

    def r_f1(g, h):
        blk = rhs.at[g, 1 - xl, ys[1], h]
        recv(("ro", g), ("-", h), blk, dev(dy=1))
        send(("rg", g), (h,), blk, blk, dev(dy=3))

    def r_done(g):
        far = ys[2]
        recv(("ry", g), ("-",), rhs.at[g, xl, ys[1]], dev(dy=1))
        recv(("rf", g), None, rhs.at[g, xl, far], dev(dy=3))
        for h in range(2):
            recv(("ro", g), ("+", h), rhs.at[g, 1 - xl, ys[3], h], dev(dy=3))
            recv(("rg", g), (h,), rhs.at[g, 1 - xl, far, h], dev(dy=1))

    def r_sent(g):
        sent(("rx", g), rhs.at[g, xl, y])
        sent(("ry", g), rhs.at[g, xl, pl.ds(0, 2)])
        sent(("ro", g), rhs.at[g, xl, pl.ds(0, 2)])
        sent(("rf", g), rhs.at[g, xl, y])
        sent(("rg", g), rhs.at[g, xl, y])

    places = [(a, c, b) for a in range(NZ) for b in range(2) for c in range(2)]

    def weights(s, which, two):
        deep = NZ if which == 1 else 4 * two + 4
        halves = []
        for m in (2 * two, 2 * two + 1):
            at = NY - 1 - m if which == 2 else m
            halves.append(jnp.concatenate([
                tab[s, c, a, at, b, 16 * which:16 * which + 16, :] if which == 1 or a // 2 <= m
                else jnp.zeros((16, 128), F32)
                for a, c, b in places if a < deep], axis=0))
        return split(jnp.concatenate(halves, axis=1))

    def part(pair_of, two):
        return tuple(v[:, :256 * two + 256] for v in pair_of)

    def blocks(g, x):
        return [rhs[g, x, j].reshape(256, 128) for j in range(NY)]

    def solve(s):
        top = split(jnp.concatenate(blocks(s, 0), axis=1))
        out = [product(part(top, two), weights(s, 0, two)) for two in range(2)]
        for j in range(4):
            xs[s, j] = out[j // 2][:, 128 * (j % 2):128 * (j % 2) + 128]
        first = split(jnp.concatenate(out, axis=1))
        out = [product(first, weights(s, 1, two)) for two in range(2)]
        rest = split(jnp.concatenate(blocks(s, 1), axis=1) - jnp.concatenate(out, axis=1))
        out = [product(part(rest, two), weights(s, 2, two)) for two in range(2)]
        for j in range(4):
            xs[s, 4 + j] = out[j // 2][:, 128 * (j % 2):128 * (j % 2) + 128]

    def whole(s):
        return split(jnp.concatenate([xs[s, j] for j in range(8)], axis=1))

    def emit(s):
        x_out[s] = xs[s, row].T

    def r_first():
        rhs[0, xl, y] = bs[0].T.reshape(2, 128, 128)

    def r_next():
        r_done(0)
        t_done(0)
        c_done()
        solve(0)
        low_cross = split(jnp.concatenate([crs[c, b, a] for a, c, b in places], axis=0))
        rhs[1, xl, y] = (bs[1].T - product(whole(0), low_cross)).reshape(2, 128, 128)

    def trail_first(i):
        if i == 0:
            emit(0)
        ats = []
        for h in (-i, i + 1):
            at = zrel(h if h >= 0 else NZ + h)
            recv(("lk", 0), (h,), lf.at[0, at, 1 - k], dev(dk=1))
            ats.append(at)
        first = split(jnp.concatenate([xs[0, at] for at in ats], axis=1))

        @pl.loop(0, 4)
        def _(j):
            lane = pl.ds(pl.multiple_of(j * 256, 256), 256)
            right = split(jnp.concatenate([lf[0, at, c, b, :, lane] for at in ats for b in range(2) for c in range(2)], axis=0))
            out = product(first, right)
            acc[j] = out if i == 0 else acc[j] + out

    def finish():
        r_done(1)
        t_done(1)
        solve(1)
        emit(1)
        l_done(1)
        second = whole(1)
        loads[10].wait()
        for j in range(4):
            at = slice(256 * j, 256 * j + 256)
            right = split(jnp.concatenate([lf[1, a, c, b, :, at] for a, c, b in places], axis=0))
            t_out[at, :] = bt[at, :] - (acc[j] + product(second, right)).T

    for step, *at in ORDER:
        {
            "tz": t_zsend, "tx": t_x, "ty": t_y, "tf": t_f, "tk": t_k, "cz": c_z, "cx": c_x, "ck": c_k,
            "load": l_load, "pair": l_pair, "hop": l_hop, "cross": l_cross, "rs": r_send, "ro": r_other, "r0": r_f0, "r1": r_f1,
            "first": r_first, "next": r_next, "trail": trail_first, "finish": finish,
        }[step](*at)
    for g in range(2):
        t_sent(g)
        r_sent(g)
    c_sent()
    l_sent()
    assert len(ids) <= N_RECV and len(streams) <= N_SEND, (len(ids), len(streams))


def shards(b_steps, b_trail, cross, trail, inv, low):
    anywhere = pl.BlockSpec(memory_space=pl.ANY)
    return pl.pallas_call(
        kernel,
        out_shape=(pltpu.VMEM((2, 128, 256), F32), pltpu.VMEM((1024, 256), F32)),
        in_specs=[anywhere] * 6,
        out_specs=(pl.BlockSpec(memory_space=pltpu.VMEM), pl.BlockSpec(memory_space=pltpu.VMEM)),
        scratch_shapes=[
            pltpu.VMEM((2, NZ, 2, 2, 32, 1024), F32),
            pltpu.VMEM((2, 2, NZ, NY, 2, 48, 128), F32),
            pltpu.VMEM((2, 2, NZ, 32, 128), F32),
            pltpu.VMEM((2, 2, NY, 2, 128, 128), F32),
            pltpu.VMEM((2, 8, 256, 128), F32),
            pltpu.VMEM((4, 256, 256), F32),
            pltpu.VMEM((2, 128, 256), F32),
            pltpu.VMEM((1024, 256), F32),
            pltpu.SemaphoreType.DMA((N_SEND,)),
            pltpu.SemaphoreType.DMA((N_RECV,)),
            pltpu.SemaphoreType.DMA((11,)),
        ],
        compiler_params=pltpu.CompilerParams(
            collective_id=0, has_side_effects=True, vmem_limit_bytes=57 << 20),
    )(
        b_steps, b_trail, cross.T, jnp.swapaxes(trail, 1, 2),
        jnp.swapaxes(inv, 2, 3), jnp.swapaxes(low, 1, 2),
    )


def solution(mesh):
    placed = (
        P(None, "row", "col"),
        P("row", "col"),
        P("row", "col"),
        P(None, "row", "col"),
        P(None, None, None, "col"),
        P(None, None, "col"),
    )
    return jax.shard_map(
        shards,
        mesh=mesh,
        in_specs=placed,
        out_specs=(P(None, "row", "col"), P("row", "col")),
        check_vma=False,
    )
```

time: 73 us -> 68 us (0.932)
  local copies, waits for them, and re-layouts: 3.93 us -> 1.67 us
  Pallas kernels: 67.8 us -> 65.6 us
    pallas_call x1, Pallas kernels: 67.8 us -> 65.6 us  [shards(): pl.pallas_call(kernel, out_shape=(pltpu.VMEM((2, 128, 256), F32), pltpu.V...]
    unnamed x2, local copies, waits for them, and re-layouts: 3.93 us -> 1.67 us
where the time goes in v4:
time: 68 us; the launch traced here: 67.9 us
  Pallas kernels  65.6 us (96%)
  local copies, waits for them, and re-layouts  1.67 us (2%)
    pallas_call x1, Pallas kernels, shards(): pl.pallas_call(kernel, out_shape=(pltpu.VMEM((2, 128, 256), F32), pltpu.V...  65.6 us
    unnamed x2, local copies, waits for them, and re-layouts  1.67 us

profile of v4, /device:TPU:1, one launch (start us, length us, event | category | flops | bytes accessed | tf_op | source)
XLA Modules:
  0.0 67.9 jit_solution(15277211781033378634)
XLA Ops:
  0.6 65.6 %shard_map.77 = (f32[2,128,256]{2,1,0:T(8,128)S(1)}, f32[1024,256]{1,0:T(8,128)S(1)}) custom-call(f32[2,128,256]{2,1,0:T(8,128)} %b_steps.1, f32[1024,256]{1,0:T(8,128)} %b_trail.1, f32[32,128]{1,0:T(8,128)} %bitcast.7, f32[2,32,1024]{2,1,0:T(8,128)} %bitcast.4, f32[2,2,16,512]{3,2,1,0:T(8,128)} %bitcast.5, f32[2,16,512]{2,1,0:T(8,128)} %bitcast.6), custom_call_target="tpu_custom_call" | custom-call | tf_op jit(solution)/shard_map/pallas_call | solution.py:394
  66.2 0.7 %copy.10 = f32[2,128,256]{2,1,0:T(8,128)} copy(f32[2,128,256]{2,1,0:T(8,128)S(1)} %get-tuple-element.2) | data formatting | bytes 524288
  66.9 1.0 %copy.11 = f32[1024,256]{1,0:T(8,128)} copy(f32[1024,256]{1,0:T(8,128)S(1)} %get-tuple-element.3) | data formatting | bytes 2097152

commit v5 on v4

--- a/solution.py
+++ b/solution.py
@@ -10,24 +10,27 @@
 BF16 = jnp.bfloat16
 
 NY, NZ = 4, 8
+PAIRED = (-1,)
 PAIRS = (0, 1, 3, 2)
-N_SEND, N_RECV = 72, 136
+N_SEND, N_RECV = 72, 128
 
 ORDER = (
-    ("tz", 0), ("first",), ("rs", 0), ("cz",), ("tx", 0, 0), ("tx", 0, 3), ("tx", 0, 1), ("ro", 0, 0), ("tx", 0, 2),
-    ("r0", 0), ("ro", 0, 1), ("ty", 0, 0), ("load",), ("hop", 1, 0, -1), ("tz", 1), ("r1", 0, 0), ("ty", 0, 3),
-    ("hop", 1, 0, 1), ("cx",), ("ty", 0, 1), ("r1", 0, 1), ("ty", 0, 2), ("tx", 1, 0), ("tx", 1, 3), ("tf", 0, 0, -1),
-    ("hop", 1, 1, -1), ("pair",), ("hop", 0, 0, -1), ("hop", 0, 0, 1), ("tx", 1, 1), ("tf", 0, 0, 1),
-    ("tf", 0, 3, -1), ("tx", 1, 2), ("tf", 0, 3, 1), ("hop", 1, 1, 1), ("tf", 0, 1, -1), ("cross", 1, 0, 1),
-    ("tf", 0, 1, 1), ("hop", 1, 2, -1), ("tf", 0, 2, 1), ("tf", 0, 2, -1), ("ck",), ("tk", 0, 0), ("ty", 1, 0),
-    ("tk", 0, 3), ("ty", 1, 3), ("hop", 0, 1, 1), ("tk", 0, 1), ("tk", 0, 2), ("hop", 0, 1, -1), ("tf", 1, 0, 1),
-    ("cross", 1, 1, -1), ("hop", 1, 2, 1), ("tf", 1, 0, -1), ("ty", 1, 1), ("next",), ("rs", 1), ("hop", 1, 3, -1),
-    ("tk", 1, 0), ("tf", 1, 3, 1), ("ty", 1, 2), ("tf", 1, 3, -1), ("trail", 0), ("cross", 1, 1, 1), ("tf", 1, 1, -1),
-    ("tf", 1, 1, 1), ("hop", 0, 2, 1), ("trail", 1), ("r0", 1), ("hop", 0, 2, -1), ("hop", 1, 3, 1),
-    ("cross", 1, 2, -1), ("tf", 1, 2, -1), ("tf", 1, 2, 1), ("hop", 1, 4, -1), ("tk", 1, 3), ("cross", 1, 2, 1),
-    ("tk", 1, 1), ("ro", 1, 0), ("hop", 0, 3, 1), ("ro", 1, 1), ("tk", 1, 2), ("r1", 1, 0), ("trail", 2),
-    ("hop", 0, 3, -1), ("cross", 1, 3, -1), ("r1", 1, 1), ("cross", 1, 3, 1), ("hop", 0, 4, 1), ("cross", 1, 4, -1),
-    ("trail", 3), ("finish",),
+    ("tz",), ("first",), ("rs", 0), ("ring", 0, -1), ("load",), ("hop", 1, 0, -1), ("ring", 0, 1), ("tx", 0, 0),
+    ("tx", 0, 3), ("tx", 0, 1), ("ro", 0, 0), ("tx", 0, 2), ("r0", 0), ("ro", 0, 1), ("ring", 1, 1), ("ring", 1, -1),
+    ("tx", 1, 0), ("r1", 0, 0), ("ring", 2, 1), ("hop", 1, 0, 1), ("pair",), ("hop", 0, 0, -1), ("r1", 0, 1),
+    ("ty", 0, 0), ("ring", 2, -1), ("ty", 0, 3), ("ring", 3, 1), ("tx", 1, 3), ("ty", 0, 1), ("hop", 0, 0, 1),
+    ("ty", 0, 2), ("ty", 1, 0), ("tf", 0, 0, 1), ("hop", 1, 1, -1), ("tf", 0, 0, -1), ("hop", 1, 1, 1),
+    ("ring", 4, 1), ("tf", 0, 3, 1), ("tf", 0, 3, -1), ("cross", 1, 0, 1), ("hop", 0, 1, -1), ("tf", 0, 1, 1),
+    ("ring", 3, -1), ("cx",), ("tx", 1, 1), ("tf", 0, 1, -1), ("ty", 1, 3), ("tx", 1, 2), ("tf", 0, 2, 1),
+    ("tf", 0, 2, -1), ("tf", 1, 0, 1), ("hop", 1, 2, -1), ("cross", 1, 1, 1), ("tf", 1, 0, -1), ("hop", 0, 1, 1),
+    ("tk", 0, 0), ("tk", 0, 3), ("cross", 1, 1, -1), ("tk", 0, 1), ("hop", 1, 2, 1), ("ck",), ("tf", 1, 3, 1),
+    ("ty", 1, 1), ("tf", 1, 3, -1), ("ty", 1, 2), ("tk", 0, 2), ("tk", 1, 0), ("next",), ("rs", 1), ("hop", 0, 2, 1),
+    ("hop", 0, 2, -1), ("tk", 1, 3), ("cross", 1, 2, -1), ("tf", 1, 1, -1), ("tf", 1, 1, 1), ("tf", 1, 2, 1),
+    ("tf", 1, 2, -1), ("trail", 0, 0), ("hop", 1, 3, -1), ("cross", 1, 2, 1), ("hop", 1, 3, 1), ("trail", 0, 1),
+    ("ro", 1, 0), ("r0", 1), ("ro", 1, 1), ("tk", 1, 1), ("tk", 1, 2), ("hop", 0, 3, 1), ("hop", 0, 3, -1),
+    ("r1", 1, 0), ("cross", 1, 3, -1), ("r1", 1, 1), ("trail", 0, 2), ("hop", 1, 4, -1), ("cross", 1, 3, 1),
+    ("last",), ("trail", 1, 0), ("hop", 0, 4, 1), ("trail", 1, 1), ("cross", 1, 4, -1), ("trail", 1, 2),
+    ("trail", 0, 3), ("finish",),
 )
 
 
@@ -55,11 +58,16 @@
     pairs = [lax.rem(lax.div(z, 2) + i, NZ // 2) for i in range(NZ // 2)]
     beside = z + 1 - 2 * lax.rem(z, 2)
 
+    places_of = {}
+
     def dev(dxl=0, dy=0, dz=0, dxh=0, dk=0):
-        a = (1 - xl) if dxl else xl
-        b = (1 - xh) if dxh else xh
-        c = (1 - k) if dk else k
-        return (a * NY + ys[dy % NY], zs_at[dz % NZ] * 4 + b * 2 + c)
+        return places_of[dxl, dy % NY, dz % NZ, dxh, dk]
+
+    def greet(dxl=0, dy=0, dz=0, dxh=0, dk=0):
+        at_row = ((1 - xl) if dxl else xl) * NY + ys[dy]
+        at_col = zs_at[dz] * 4 + ((1 - xh) if dxh else xh) * 2 + ((1 - k) if dk else k)
+        places_of[dxl, dy, dz, dxh, dk] = (at_row, at_col)
+        return at_row, at_col
 
     ids, streams = {}, {}
 
@@ -69,10 +77,10 @@
     def out_sem(stream):
         return streams.setdefault(stream, len(streams))
 
-    def send(stream, at, src, dst, to_dev):
+    def send(stream, at, src, dst, to_dev, rs_name=None):
         pltpu.make_async_remote_copy(
             src_ref=src, dst_ref=dst, send_sem=ss.at[out_sem(stream)],
-            recv_sem=rs.at[sem(stream) if at is None else sem((stream, at))],
+            recv_sem=rs.at[sem(rs_name or (stream if at is None else (stream, at)))],
             device_id=to_dev, device_id_type=MESH).start()
 
     def recv(stream, at, region, from_dev):
@@ -86,7 +94,7 @@
             src_ref=region, dst_ref=region, send_sem=ss.at[streams[stream]], recv_sem=rs.at[0],
             device_id=dev(dk=1), device_id_type=MESH).wait_send()
 
-    partners = [dev(dz=e) for e in range(1, NZ)] + [dev(dy=1), dev(dy=3), dev(dxl=1), dev(dxh=1), dev(dk=1)]
+    partners = [greet(dz=e) for e in range(1, NZ)] + [greet(dy=1), greet(dy=3), greet(dxl=1), greet(dxh=1), greet(dk=1)]
     barrier = pltpu.get_barrier_semaphore()
     for p in partners:
         pl.semaphore_signal(barrier, inc=1, device_id=p, device_id_type=MESH)
@@ -114,34 +122,49 @@
 
     def filled(zz, at_y, act):
         p, q = zz <= at_y, zz <= NY - 1 - at_y
-        for rows, when in (
-            (pl.ds(0, 48), p & q),
-            (pl.ds(0, 32), p & (zz > NY - 1 - at_y)),
-            (pl.ds(16, 32), (zz > at_y) & q),
-            (pl.ds(16, 16), (zz > at_y) & (zz > NY - 1 - at_y)),
-        ):
-            pl.when(when)(lambda rows=rows: act(rows))
+        lax.cond(
+            p,
+            lambda: lax.cond(q, lambda: act(pl.ds(0, 48)), lambda: act(pl.ds(0, 32))),
+            lambda: lax.cond(q, lambda: act(pl.ds(16, 32)), lambda: act(pl.ds(16, 16))),
+        )
 
     def pair(d):
         return pairs[d]
 
-    tz = [[sem(("tz", g, e)) for e in range(NZ)] for g in range(2)]
-
-    def t_zsend(g):
-        def act(rows):
-            blk = tab.at[g, k, z, y, xh, rows]
+    tz = [sem(("tz", e)) for e in range(NZ)]
+
+    def t_zsend():
+        def act(rows):
+            blk = tab.at[0, k, z, y, xh, rows]
             for e in range(1, NZ):
                 pltpu.make_async_remote_copy(
-                    src_ref=blk, dst_ref=blk, send_sem=ss.at[out_sem(("tz", g))], recv_sem=rs.at[tz[g][e]],
+                    src_ref=blk, dst_ref=blk, send_sem=ss.at[out_sem("tz")], recv_sem=rs.at[tz[e]],
                     device_id=dev(dz=e), device_id_type=MESH).start()
         filled(pairs[0], y, act)
 
+    def ring(h, sign):
+        at = zrel(h if sign > 0 else NZ - h)
+        last = h == (4 if sign > 0 else 3)
+        blk = crs.at[k, xh, at]
+        if h:
+            recv("cr", (sign, h), blk, dev(dz=NZ - sign))
+        if not last:
+            send("cr", (sign, h + 1), blk, blk, dev(dz=sign % NZ))
+
+        def act(rows):
+            blk = tab.at[1, k, at, y, xh, rows]
+            if h:
+                recv(("tr", sign), (h,), blk, dev(dz=NZ - sign))
+            if not last:
+                send(("tr", sign, h), None, blk, blk, dev(dz=sign % NZ), rs_name=(("tr", sign), (h + 1,)))
+        filled(lax.div(at, 2), y, act)
+
     def t_x(g, d):
         def act(rows):
             zz = pair(d)
-            for from_z in [2 * zz, 2 * zz + 1] if d else [beside]:
+            for from_z in () if g else (2 * zz, 2 * zz + 1) if d else (beside,):
                 e = lax.rem(z - from_z + NZ, NZ)
-                recv(("tz", g), tz[g][0] + e, tab.at[g, k, from_z, y, xh, rows], dev(dz=1))
+                recv("tz", tz[0] + e, tab.at[g, k, from_z, y, xh, rows], dev(dz=1))
             blk = tab.at[g, k, pl.ds(2 * zz, 2), y, xh, rows]
             send(("tx", g, d), None, blk, blk, dev(dxh=1))
         filled(pair(d), y, act)
@@ -181,7 +204,13 @@
         recv(("tk", g), None, tab.at[g, 1 - k], dev(dk=1))
 
     def t_sent(g):
-        filled(pairs[0], y, lambda rows: sent(("tz", g), tab.at[g, k, pl.ds(0, NZ - 1), y, xh, rows]))
+        if g == 0:
+            filled(pairs[0], y, lambda rows: sent("tz", tab.at[g, k, pl.ds(0, NZ - 1), y, xh, rows]))
+        else:
+            for sign, last in ((1, 4), (-1, 3)):
+                for h in range(last):
+                    at = zrel(h if sign > 0 else NZ - h)
+                    filled(lax.div(at, 2), y, lambda rows: sent(("tr", sign, h), tab.at[g, k, at, y, xh, rows]))
         for d in PAIRS:
             zs = pl.ds(2 * pair(d), 2)
 
@@ -194,13 +223,7 @@
                 filled(pair(d), near, lambda rows: sent(("tf" + name, g, d), tab.at[g, k, zs, near, 0, rows]))
         sent(("tk", g), tab.at[g, k])
 
-    def c_z():
-        blk = crs.at[k, xh, z]
-        for e in range(1, NZ):
-            send("cz", None, blk, blk, dev(dz=e))
-
     def c_x():
-        recv("cz", None, crs.at[k, xh, pl.ds(0, NZ - 1)], dev(dz=1))
         send("cx", None, crs.at[k, xh], crs.at[k, xh], dev(dxh=1))
 
     def c_k():
@@ -211,7 +234,7 @@
         recv("ck", None, crs.at[1 - k], dev(dk=1))
 
     def c_sent():
-        sent("cz", crs.at[k, xh, pl.ds(0, NZ - 1)])
+        sent("cr", crs.at[k, xh, pl.ds(0, NZ - 1)])
         sent("cx", crs.at[k, xh])
         sent("ck", crs.at[k])
 
@@ -239,22 +262,29 @@
         if s == 0:
             send(("lk", s), (sign * h,), blk, blk, dev(dk=1))
         else:
-            send(("lx", s), (sign * h,), blk, blk, dev(dxh=1))
+            if not (h == 1 and sign in PAIRED):
+                send(("lx", s), (sign * h,), blk, blk, dev(dxh=1))
 
     def l_cross(s, h, sign):
         at = zrel(h if sign > 0 else NZ - h)
-        recv(("lx", s), (sign * h,), lf.at[s, at, k, 1 - xh], dev(dxh=1))
+        blk = lf.at[s, at, k, 1 - xh]
+        if h == 1 and sign in PAIRED:
+            recv("lp", (sign,), blk, dev(dz=NZ - sign))
+        else:
+            recv(("lx", s), (sign * h,), blk, dev(dxh=1))
+        if h == 0:
+            for side in PAIRED:
+                send("lp", (side,), blk, blk, dev(dz=side % NZ))
         blk = lf.at[s, at, k]
-        send(("lk", s), None, blk, blk, dev(dk=1))
-
-    def l_done(s):
-        recv(("lk", s), None, lf.at[s, :, 1 - k], dev(dk=1))
+        send(("lk", s), (sign * h,), blk, blk, dev(dk=1))
 
     def l_sent():
         sent("l0x", lf.at[0, z, k, xh])
         sent(("l", 0), lf.at[0, pl.ds(0, NZ - 1), k])
         sent(("l", 1), lf.at[1, pl.ds(0, NZ - 1), k, xh])
-        sent(("lx", 1), lf.at[1, :, k, xh])
+        sent(("lx", 1), lf.at[1, pl.ds(0, NZ - len(PAIRED)), k, xh])
+        if PAIRED:
+            sent("lp", lf.at[1, pl.ds(0, len(PAIRED)), k, xh])
         for s in range(2):
             sent(("lk", s), lf.at[s, :, k])
 
@@ -345,41 +375,44 @@
         low_cross = split(jnp.concatenate([crs[c, b, a] for a, c, b in places], axis=0))
         rhs[1, xl, y] = (bs[1].T - product(whole(0), low_cross)).reshape(2, 128, 128)
 
-    def trail_first(i):
-        if i == 0:
-            emit(0)
+    def trail_part(s, i):
         ats = []
-        for h in (-i, i + 1):
+        for h in (-i, i + 1) if s == 0 else (i, -i - 1):
             at = zrel(h if h >= 0 else NZ + h)
-            recv(("lk", 0), (h,), lf.at[0, at, 1 - k], dev(dk=1))
+            recv(("lk", s), (h,), lf.at[s, at, 1 - k], dev(dk=1))
             ats.append(at)
-        first = split(jnp.concatenate([xs[0, at] for at in ats], axis=1))
+        return split(jnp.concatenate([xs[s, at] for at in ats], axis=1)), ats
+
+    def right(s, ats, lane):
+        return split(jnp.concatenate([lf[s, at, c, b, :, lane] for at in ats for b in range(2) for c in range(2)], axis=0))
+
+    def trail(s, i):
+        left, ats = trail_part(s, i)
 
         @pl.loop(0, 4)
         def _(j):
-            lane = pl.ds(pl.multiple_of(j * 256, 256), 256)
-            right = split(jnp.concatenate([lf[0, at, c, b, :, lane] for at in ats for b in range(2) for c in range(2)], axis=0))
-            out = product(first, right)
-            acc[j] = out if i == 0 else acc[j] + out
-
-    def finish():
+            out = product(left, right(s, ats, pl.ds(pl.multiple_of(j * 256, 256), 256)))
+            acc[j] = out if s == 0 and i == 0 else acc[j] + out
+
+    def solve_last():
+        emit(0)
         r_done(1)
         t_done(1)
         solve(1)
         emit(1)
-        l_done(1)
-        second = whole(1)
         loads[10].wait()
+
+    def finish():
+        left, ats = trail_part(1, 3)
         for j in range(4):
             at = slice(256 * j, 256 * j + 256)
-            right = split(jnp.concatenate([lf[1, a, c, b, :, at] for a, c, b in places], axis=0))
-            t_out[at, :] = bt[at, :] - (acc[j] + product(second, right)).T
+            t_out[at, :] = bt[at, :] - (acc[j] + product(left, right(1, ats, at))).T
 
     for step, *at in ORDER:
         {
-            "tz": t_zsend, "tx": t_x, "ty": t_y, "tf": t_f, "tk": t_k, "cz": c_z, "cx": c_x, "ck": c_k,
+            "tz": t_zsend, "ring": ring, "tx": t_x, "ty": t_y, "tf": t_f, "tk": t_k, "cx": c_x, "ck": c_k,
             "load": l_load, "pair": l_pair, "hop": l_hop, "cross": l_cross, "rs": r_send, "ro": r_other, "r0": r_f0, "r1": r_f1,
-            "first": r_first, "next": r_next, "trail": trail_first, "finish": finish,
+            "first": r_first, "next": r_next, "trail": trail, "last": solve_last, "finish": finish,
         }[step](*at)
     for g in range(2):
         t_sent(g)

time: 68 us -> 65.5 us (0.963)
  Pallas kernels: 65.6 us -> 63.1 us
    pallas_call x1, Pallas kernels: 65.6 us -> 63.1 us  [shards(): pl.pallas_call(kernel, out_shape=(pltpu.VMEM((2, 128, 256), F32), pltpu.V...]
where the time goes in v5:
time: 65.5 us; the launch traced here: 65.4 us
  Pallas kernels  63.1 us (96%)
  local copies, waits for them, and re-layouts  1.67 us (3%)
    pallas_call x1, Pallas kernels, shards(): pl.pallas_call(kernel, out_shape=(pltpu.VMEM((2, 128, 256), F32), pltpu.V...  63.1 us
    unnamed x2, local copies, waits for them, and re-layouts  1.67 us

profile of v5, /device:TPU:1, one launch (start us, length us, event | category | flops | bytes accessed | tf_op | source)
XLA Modules:
  0.0 65.4 jit_solution(15227042008372798914)
XLA Ops:
  0.6 63.1 %shard_map.77 = (f32[2,128,256]{2,1,0:T(8,128)S(1)}, f32[1024,256]{1,0:T(8,128)S(1)}) custom-call(f32[2,128,256]{2,1,0:T(8,128)} %b_steps.1, f32[1024,256]{1,0:T(8,128)} %b_trail.1, f32[32,128]{1,0:T(8,128)} %bitcast.7, f32[2,32,1024]{2,1,0:T(8,128)} %bitcast.4, f32[2,2,16,512]{3,2,1,0:T(8,128)} %bitcast.5, f32[2,16,512]{2,1,0:T(8,128)} %bitcast.6), custom_call_target="tpu_custom_call" | custom-call | tf_op jit(solution)/shard_map/pallas_call | solution.py:427
  63.7 0.7 %copy.10 = f32[2,128,256]{2,1,0:T(8,128)} copy(f32[2,128,256]{2,1,0:T(8,128)S(1)} %get-tuple-element.2) | data formatting | bytes 524288
  64.4 1.0 %copy.11 = f32[1024,256]{1,0:T(8,128)} copy(f32[1024,256]{1,0:T(8,128)S(1)} %get-tuple-element.3) | data formatting | bytes 2097152

commit v6 on v5

--- a/solution.py
+++ b/solution.py
@@ -12,7 +12,7 @@
 NY, NZ = 4, 8
 PAIRED = (-1,)
 PAIRS = (0, 1, 3, 2)
-N_SEND, N_RECV = 72, 128
+N_SEND, N_RECV = 42, 128
 
 ORDER = (
     ("tz",), ("first",), ("rs", 0), ("ring", 0, -1), ("load",), ("hop", 1, 0, -1), ("ring", 0, 1), ("tx", 0, 0),
@@ -24,12 +24,12 @@
     ("ring", 3, -1), ("cx",), ("tx", 1, 1), ("tf", 0, 1, -1), ("ty", 1, 3), ("tx", 1, 2), ("tf", 0, 2, 1),
     ("tf", 0, 2, -1), ("tf", 1, 0, 1), ("hop", 1, 2, -1), ("cross", 1, 1, 1), ("tf", 1, 0, -1), ("hop", 0, 1, 1),
     ("tk", 0, 0), ("tk", 0, 3), ("cross", 1, 1, -1), ("tk", 0, 1), ("hop", 1, 2, 1), ("ck",), ("tf", 1, 3, 1),
-    ("ty", 1, 1), ("tf", 1, 3, -1), ("ty", 1, 2), ("tk", 0, 2), ("tk", 1, 0), ("next",), ("rs", 1), ("hop", 0, 2, 1),
+    ("ty", 1, 1), ("tf", 1, 3, -1), ("ty", 1, 2), ("tk", 0, 2), ("next",), ("rs", 1), ("tk", 1, 0), ("hop", 0, 2, 1),
     ("hop", 0, 2, -1), ("tk", 1, 3), ("cross", 1, 2, -1), ("tf", 1, 1, -1), ("tf", 1, 1, 1), ("tf", 1, 2, 1),
     ("tf", 1, 2, -1), ("trail", 0, 0), ("hop", 1, 3, -1), ("cross", 1, 2, 1), ("hop", 1, 3, 1), ("trail", 0, 1),
     ("ro", 1, 0), ("r0", 1), ("ro", 1, 1), ("tk", 1, 1), ("tk", 1, 2), ("hop", 0, 3, 1), ("hop", 0, 3, -1),
     ("r1", 1, 0), ("cross", 1, 3, -1), ("r1", 1, 1), ("trail", 0, 2), ("hop", 1, 4, -1), ("cross", 1, 3, 1),
-    ("last",), ("trail", 1, 0), ("hop", 0, 4, 1), ("trail", 1, 1), ("cross", 1, 4, -1), ("trail", 1, 2),
+    ("last",), ("trail", 1, 0), ("hop", 0, 4, 1), ("trail", 1, 1), ("early",), ("cross", 1, 4, -1), ("trail", 1, 2),
     ("trail", 0, 3), ("finish",),
 )
 
@@ -166,17 +166,17 @@
                 e = lax.rem(z - from_z + NZ, NZ)
                 recv("tz", tz[0] + e, tab.at[g, k, from_z, y, xh, rows], dev(dz=1))
             blk = tab.at[g, k, pl.ds(2 * zz, 2), y, xh, rows]
-            send(("tx", g, d), None, blk, blk, dev(dxh=1))
+            send(("tx", g), (d,), blk, blk, dev(dxh=1))
         filled(pair(d), y, act)
 
     def t_y(g, d):
         zs = pl.ds(2 * pair(d), 2)
 
         def act(rows):
-            recv(("tx", g, d), None, tab.at[g, k, zs, y, 1 - xh, rows], dev(dxh=1))
+            recv(("tx", g), (d,), tab.at[g, k, zs, y, 1 - xh, rows], dev(dxh=1))
             blk = tab.at[g, k, zs, y, :, rows]
-            send(("ty+", g, d), None, blk, blk, dev(dy=1))
-            send(("ty-", g, d), None, blk, blk, dev(dy=3))
+            send(("ty+", g), (d,), blk, blk, dev(dy=1))
+            send(("ty-", g), (d,), blk, blk, dev(dy=3))
         filled(pair(d), y, act)
 
     def t_f(g, d, sign):
@@ -184,9 +184,9 @@
         name, near, half = ("+", ys[3], 0) if sign > 0 else ("-", ys[1], 1)
 
         def act(rows):
-            recv(("ty" + name, g, d), None, tab.at[g, k, zs, near, :, rows], dev(dy=NY - sign))
+            recv(("ty" + name, g), (d,), tab.at[g, k, zs, near, :, rows], dev(dy=NY - sign))
             blk = tab.at[g, k, zs, near, half, rows]
-            send(("tf" + name, g, d), None, blk, blk, dev(dy=sign % NY))
+            send(("tf" + name, g), (d,), blk, blk, dev(dy=sign % NY))
         filled(pair(d), near, act)
 
     def t_k(g, d):
@@ -194,8 +194,8 @@
         far = ys[2]
 
         def act(rows):
-            recv(("tf+", g, d), None, tab.at[g, k, zs, far, 0, rows], dev(dy=3))
-            recv(("tf-", g, d), None, tab.at[g, k, zs, far, 1, rows], dev(dy=1))
+            recv(("tf+", g), (d,), tab.at[g, k, zs, far, 0, rows], dev(dy=3))
+            recv(("tf-", g), (d,), tab.at[g, k, zs, far, 1, rows], dev(dy=1))
         filled(pair(d), far, act)
         blk = tab.at[g, k, zs]
         send(("tk", g), None, blk, blk, dev(dk=1))
@@ -204,6 +204,7 @@
         recv(("tk", g), None, tab.at[g, 1 - k], dev(dk=1))
 
     def t_sent(g):
+        six = pl.ds(0, 6)
         if g == 0:
             filled(pairs[0], y, lambda rows: sent("tz", tab.at[g, k, pl.ds(0, NZ - 1), y, xh, rows]))
         else:
@@ -211,16 +212,10 @@
                 for h in range(last):
                     at = zrel(h if sign > 0 else NZ - h)
                     filled(lax.div(at, 2), y, lambda rows: sent(("tr", sign, h), tab.at[g, k, at, y, xh, rows]))
-        for d in PAIRS:
-            zs = pl.ds(2 * pair(d), 2)
-
-            def act(rows):
-                sent(("tx", g, d), tab.at[g, k, zs, y, xh, rows])
-                sent(("ty+", g, d), tab.at[g, k, zs, y, :, rows])
-                sent(("ty-", g, d), tab.at[g, k, zs, y, :, rows])
-            filled(pair(d), y, act)
-            for name, near in (("+", ys[3]), ("-", ys[1])):
-                filled(pair(d), near, lambda rows: sent(("tf" + name, g, d), tab.at[g, k, zs, near, 0, rows]))
+        sent(("tx", g), tab.at[g, k, six, y, xh])
+        for sign in "+-":
+            sent(("ty" + sign, g), tab.at[g, k, six, y])
+            sent(("tf" + sign, g), tab.at[g, k, six, y, xh])
         sent(("tk", g), tab.at[g, k])
 
     def c_x():
@@ -402,7 +397,14 @@
         emit(1)
         loads[10].wait()
 
+    def early():
+        t_sent(0)
+        r_sent(0)
+        c_sent()
+        t_sent(1)
+
     def finish():
+        r_sent(1)
         left, ats = trail_part(1, 3)
         for j in range(4):
             at = slice(256 * j, 256 * j + 256)
@@ -412,12 +414,8 @@
         {
             "tz": t_zsend, "ring": ring, "tx": t_x, "ty": t_y, "tf": t_f, "tk": t_k, "cx": c_x, "ck": c_k,
             "load": l_load, "pair": l_pair, "hop": l_hop, "cross": l_cross, "rs": r_send, "ro": r_other, "r0": r_f0, "r1": r_f1,
-            "first": r_first, "next": r_next, "trail": trail, "last": solve_last, "finish": finish,
+            "first": r_first, "next": r_next, "trail": trail, "last": solve_last, "early": early, "finish": finish,
         }[step](*at)
-    for g in range(2):
-        t_sent(g)
-        r_sent(g)
-    c_sent()
     l_sent()
     assert len(ids) <= N_RECV and len(streams) <= N_SEND, (len(ids), len(streams))
 

time: 65.5 us -> 64.6 us (0.986)
  Pallas kernels: 63.1 us -> 62.2 us
    pallas_call x1, Pallas kernels: 63.1 us -> 62.2 us  [shards(): pl.pallas_call(kernel, out_shape=(pltpu.VMEM((2, 128, 256), F32), pltpu.V...]
where the time goes in v6:
time: 64.6 us; the launch traced here: 64.5 us
  Pallas kernels  62.2 us (96%)
  local copies, waits for them, and re-layouts  1.67 us (3%)
    pallas_call x1, Pallas kernels, shards(): pl.pallas_call(kernel, out_shape=(pltpu.VMEM((2, 128, 256), F32), pltpu.V...  62.2 us
    unnamed x2, local copies, waits for them, and re-layouts  1.67 us

profile of v6, /device:TPU:1, one launch (start us, length us, event | category | flops | bytes accessed | tf_op | source)
XLA Modules:
  0.0 64.5 jit_solution(14404210316349248495)
XLA Ops:
  0.6 62.2 %shard_map.77 = (f32[2,128,256]{2,1,0:T(8,128)S(1)}, f32[1024,256]{1,0:T(8,128)S(1)}) custom-call(f32[2,128,256]{2,1,0:T(8,128)} %b_steps.1, f32[1024,256]{1,0:T(8,128)} %b_trail.1, f32[32,128]{1,0:T(8,128)} %bitcast.7, f32[2,32,1024]{2,1,0:T(8,128)} %bitcast.4, f32[2,2,16,512]{3,2,1,0:T(8,128)} %bitcast.5, f32[2,16,512]{2,1,0:T(8,128)} %bitcast.6), custom_call_target="tpu_custom_call" | custom-call | tf_op jit(solution)/shard_map/pallas_call | solution.py:425
  62.9 0.7 %copy.10 = f32[2,128,256]{2,1,0:T(8,128)} copy(f32[2,128,256]{2,1,0:T(8,128)S(1)} %get-tuple-element.2) | data formatting | bytes 524288
  63.6 1.0 %copy.11 = f32[1024,256]{1,0:T(8,128)} copy(f32[1024,256]{1,0:T(8,128)S(1)} %get-tuple-element.3) | data formatting | bytes 2097152

commit v7 on v6

--- a/solution.py
+++ b/solution.py
@@ -405,6 +405,7 @@
 
     def finish():
         r_sent(1)
+        l_sent()
         left, ats = trail_part(1, 3)
         for j in range(4):
             at = slice(256 * j, 256 * j + 256)
@@ -416,7 +417,6 @@
             "load": l_load, "pair": l_pair, "hop": l_hop, "cross": l_cross, "rs": r_send, "ro": r_other, "r0": r_f0, "r1": r_f1,
             "first": r_first, "next": r_next, "trail": trail, "last": solve_last, "early": early, "finish": finish,
         }[step](*at)
-    l_sent()
     assert len(ids) <= N_RECV and len(streams) <= N_SEND, (len(ids), len(streams))
 
 

time: 64.6 us -> 64.6 us (level)
  no operation moved by 1% of the time
where the time goes in v7:
time: 64.6 us
  Pallas kernels  62.2 us (96%)
  local copies, waits for them, and re-layouts  1.67 us (3%)
    pallas_call x1, Pallas kernels, shards(): pl.pallas_call(kernel, out_shape=(pltpu.VMEM((2, 128, 256), F32), pltpu.V...  62.2 us
    unnamed x2, local copies, waits for them, and re-layouts  1.67 us

profile of v7, /device:TPU:1, one launch (start us, length us, event | category | flops | bytes accessed | tf_op | source)
XLA Modules:
  0.0 64.6 jit_solution(10048102703062501241)
XLA Ops:
  0.6 62.2 %shard_map.77 = (f32[2,128,256]{2,1,0:T(8,128)S(1)}, f32[1024,256]{1,0:T(8,128)S(1)}) custom-call(f32[2,128,256]{2,1,0:T(8,128)} %b_steps.1, f32[1024,256]{1,0:T(8,128)} %b_trail.1, f32[32,128]{1,0:T(8,128)} %bitcast.7, f32[2,32,1024]{2,1,0:T(8,128)} %bitcast.4, f32[2,2,16,512]{3,2,1,0:T(8,128)} %bitcast.5, f32[2,16,512]{2,1,0:T(8,128)} %bitcast.6), custom_call_target="tpu_custom_call" | custom-call | tf_op jit(solution)/shard_map/pallas_call | solution.py:425
  62.9 0.7 %copy.10 = f32[2,128,256]{2,1,0:T(8,128)} copy(f32[2,128,256]{2,1,0:T(8,128)S(1)} %get-tuple-element.2) | data formatting | bytes 524288
  63.6 1.0 %copy.11 = f32[1024,256]{1,0:T(8,128)} copy(f32[1024,256]{1,0:T(8,128)S(1)} %get-tuple-element.3) | data formatting | bytes 2097152
